TPU v7x, 32 devices: a whole 2x2x4 slice. The times are simulated.
32 devices in a mesh: wide: 8 (over z, y), narrow: 4 (over x, core).
Axes of the slice: x: 2, y: 2, z: 4, core: 2. Of those that a mesh axis runs over, the one named last changes fastest.
Arguments:
- tokens: bfloat16 [9344, 768], P('wide'), may hold values from -6 to 6
- w_qkv: bfloat16 [3, 768, 768], P(None, None, 'narrow'), may hold values from -0.21875 to 0.21875
- qv_bias: bfloat16 [2, 768], P(None, 'narrow'), may hold values from -1.75 to 1.75
- w_proj: bfloat16 [768, 768], P('narrow'), may hold values from -1.75 to 1.75
- proj_bias: bfloat16 [768], replicated, may hold values from -1.75 to 1.75
- w_fc1: bfloat16 [768, 3072], P(None, 'narrow'), may hold values from -0.21875 to 0.21875
- fc1_bias: bfloat16 [3072], P('narrow'), may hold values from -1.75 to 1.75
- w_fc2: bfloat16 [3072, 768], P('narrow'), may hold values from -0.109375 to 0.109375
- fc2_bias: bfloat16 [768], replicated, may hold values from -1.75 to 1.75
- norm_gains: bfloat16 [2, 768], replicated, may hold values from 0.5 to 1.5
- norm_shifts: bfloat16 [2, 768], replicated, may hold values from -1.75 to 1.75
- layer_scales: bfloat16 [2, 768], replicated, may hold values from 0.5 to 2
- rel_table: bfloat16 [12, 2212], P('narrow'), may hold values from -6 to 6
- image_ids: int32 [9344], P('wide'), may hold values from 0 to 31, as said below
- pad_mask: int32 [9344], P('wide'), may hold values from 0 to 1, as said below
- grid_rows: int32 [9344], P('wide'), may hold values from -1 to 23, as said below
- grid_cols: int32 [9344], P('wide'), may hold values from -1 to 23, as said below
- d_out: bfloat16 [9344, 768], P('wide'), may hold values from -6 to 6
Outputs:
- block_out: bfloat16 [9344, 768], P('wide')
- d_tokens: float32 [9344, 768], P('wide')
- d_qkv: float32 [3, 768, 768], P(None, None, 'narrow')
- d_qv_bias: float32 [2, 768], P(None, 'narrow')
- d_proj: float32 [768, 768], P('narrow')
- d_proj_bias: float32 [768], replicated
- d_fc1: float32 [768, 3072], P(None, 'narrow')
- d_fc1_bias: float32 [3072], P('narrow')
- d_fc2: float32 [3072, 768], P('narrow')
- d_fc2_bias: float32 [768], replicated
- d_norm_gains: float32 [2, 768], replicated
- d_norm_shifts: float32 [2, 768], replicated
- d_layer_scales: float32 [2, 768], replicated
- d_rel_table: float32 [12, 2212], P('narrow')
Inputs may be any that keep to these rules, and one draw needn't show every extreme that they name: `image_ids`: each aligned block of 584 rows, number b, holds either one image of 24 x 24 patches with id 2 * b, or two images of 14 x 14 patches with ids 2 * b and 2 * b + 1 whose slots start at rows 0 and 208 of the block; padding slots carry the id of the image before them; block 0 is of the first kind, block 1 and the last block of the second. `pad_mask`: each image's first slot is its class token, followed by its patches row by row; all later slots of the image are padding. `grid_rows`: padding slots have coordinates 0. `grid_cols`: padding slots have coordinates 0.
All inputs are finite; a program needn't handle non-finite values.
Results may differ from a plain program's by a relative error of at most 0.012.
Values sent between devices are 32-bit elements; how exact they have to be, the bound alone decides.
No kernel may reach another device: no remote copies, remote signals or barrier semaphores. Data moves between devices by JAX's collectives and lax.ppermute only.
A program may use at most 192 MiB of HBM per device.

v0:
```python
from functools import partial

import jax
import jax.numpy as jnp
import numpy as np
from jax import lax
from jax.sharding import PartitionSpec as P

HD = 64
GRID = 24
LONG = 584


EPSILON = 1e-06


def normalize(values, gain_row, shift_row):
    row_mean = jnp.mean(values, axis=-1, keepdims=True)
    centred = values - row_mean
    inverse = lax.rsqrt(jnp.mean(centred * centred, axis=-1, keepdims=True) + EPSILON)
    unit_rows = centred * inverse
    return (unit_rows * gain_row + shift_row, unit_rows, inverse)


def normalize_back(upstream, unit_rows, inverse, gain_row):
    scaled = upstream * gain_row
    centred = scaled - jnp.mean(scaled, axis=-1, keepdims=True)
    centred = centred - unit_rows * jnp.mean(scaled * unit_rows, axis=-1, keepdims=True)
    return (inverse * centred, jnp.sum(upstream * unit_rows, axis=0), jnp.sum(upstream, axis=0))


def offset_table():
    grid_side = 2 * GRID - 1
    coords = np.arange(GRID)
    differ = coords[:, None] - coords[None, :] + GRID - 1
    return (differ[:, :, None] == np.arange(grid_side)[None, None, :]).astype(np.float32)


def padded_cells():
    return (GRID * GRID + 1 + 127) // 128 * 128


def class_masks(padded):
    cells = np.arange(padded)
    is_patch = cells < GRID * GRID
    is_class = cells == GRID * GRID
    query_class = (is_class[:, None] & is_patch[None, :]).astype(np.float32)
    key_class = (is_patch[:, None] & is_class[None, :]).astype(np.float32)
    both_class = (is_class[:, None] & is_class[None, :]).astype(np.float32)
    return (query_class, key_class, both_class)


def expand_table(rel_table, padded):
    grid_side = 2 * GRID - 1
    relative = grid_side * grid_side
    heads = rel_table.shape[0]
    cell_count = GRID * GRID
    shift_low = jnp.asarray(offset_table(), jnp.bfloat16)
    grid_part = rel_table[:, :relative].reshape(heads, grid_side, grid_side)
    by_row = jnp.einsum(
        "rsd,hdc->hrsc", shift_low, grid_part, preferred_element_type=jnp.float32
    ).astype(jnp.bfloat16)
    patch = jnp.einsum("hrsc,abc->hrasb", by_row, shift_low, preferred_element_type=jnp.float32)
    patch = patch.reshape(heads, cell_count, cell_count)
    patch = jnp.pad(patch, ((0, 0), (0, padded - cell_count), (0, padded - cell_count)))
    tail = rel_table[:, relative : relative + 3].astype(jnp.float32)
    query_class, key_class, both_class = class_masks(padded)
    expanded = patch + jnp.asarray(query_class)[None] * tail[:, 0, None, None]
    expanded = expanded + jnp.asarray(key_class)[None] * tail[:, 1, None, None]
    expanded = expanded + jnp.asarray(both_class)[None] * tail[:, 2, None, None]
    return expanded.astype(jnp.bfloat16)


def table_back(table_grad):
    grid_side = 2 * GRID - 1
    relative = grid_side * grid_side
    heads = table_grad.shape[0]
    cell_count = GRID * GRID
    shift_full = jnp.asarray(offset_table(), jnp.float32)
    patch_grad = table_grad[:, :cell_count, :cell_count].reshape(heads, GRID, GRID, GRID, GRID)
    by_col = jnp.einsum("hrasb,abk->hrsk", patch_grad, shift_full, precision=lax.Precision.HIGHEST)
    grid_grad = jnp.einsum(
        "hrsk,rsj->hjk", by_col, shift_full, precision=lax.Precision.HIGHEST
    ).reshape(heads, relative)
    query_term = jnp.sum(table_grad[:, cell_count, :cell_count], axis=-1)
    key_term = jnp.sum(table_grad[:, :cell_count, cell_count], axis=-1)
    both_term = table_grad[:, cell_count, cell_count]
    return jnp.concatenate(
        [grid_grad, jnp.stack([query_term, key_term, both_term], axis=1)], axis=1
    )


def pack_scores(query_pack, key_pack, expanded, one_hot, image_pack, mask_pack):
    by_query = jnp.einsum(
        "qc,hce->hqe", one_hot, expanded, preferred_element_type=jnp.float32
    ).astype(jnp.bfloat16)
    pos_bias = jnp.einsum("hqe,ke->hqk", by_query, one_hot, preferred_element_type=jnp.float32)
    scores = (
        jnp.einsum("qhd,khd->hqk", query_pack, key_pack, preferred_element_type=jnp.float32)
        + pos_bias
    )
    allowed = (image_pack[:, None] == image_pack[None, :]) & (mask_pack[None, :] == 1)
    return jnp.where(allowed[None], scores, -jnp.inf)


def log_norm(scores):
    row_top = jnp.max(scores, axis=-1, keepdims=True)
    return row_top + jnp.log(jnp.sum(jnp.exp(scores - row_top), axis=-1, keepdims=True))


def on_device(
    tokens,
    w_qkv,
    qv_bias,
    w_proj,
    proj_bias,
    w_fc1,
    fc1_bias,
    w_fc2,
    fc2_bias,
    norm_gains,
    norm_shifts,
    layer_scales,
    rel_table,
    image_ids,
    pad_mask,
    grid_rows,
    grid_cols,
    d_out,
):
    row_count = tokens.shape[0]
    local_width = w_qkv.shape[2]
    local_heads = local_width // HD
    pack_count = row_count // LONG
    head_scale = HD ** (-0.5)
    gains = norm_gains.astype(jnp.float32)
    shifts = norm_shifts.astype(jnp.float32)
    scales = layer_scales.astype(jnp.float32)
    biases = qv_bias.astype(jnp.float32)
    inputs = tokens.astype(jnp.float32)
    normed_one, unit_one, inverse_one = normalize(inputs, gains[0], shifts[0])
    normed_low = normed_one.astype(jnp.bfloat16)
    projected = jnp.einsum("rd,kde->kre", normed_low, w_qkv, preferred_element_type=jnp.float32)
    query_all = ((projected[0] + biases[0]) * head_scale).astype(jnp.bfloat16)
    key_all = projected[1].astype(jnp.bfloat16)
    value_all = (projected[2] + biases[1]).astype(jnp.bfloat16)
    padded = padded_cells()
    expanded = expand_table(rel_table, padded)
    cell_rows = jnp.where(grid_rows >= 0, grid_rows * GRID + grid_cols, GRID * GRID)
    cell_grid = jnp.arange(padded, dtype=jnp.int32)
    pack_shape = (LONG, local_heads, HD)

    def pack_inputs(pack_index):
        window = slice(pack_index * LONG, (pack_index + 1) * LONG)
        one_hot = (cell_rows[window][:, None] == cell_grid[None, :]).astype(jnp.bfloat16)
        return (
            query_all[window].reshape(pack_shape),
            key_all[window].reshape(pack_shape),
            value_all[window].reshape(pack_shape),
            one_hot,
            image_ids[window],
            pad_mask[window],
        )

    head_list = []
    norm_list = []
    for pack_index in range(pack_count):
        query_pack, key_pack, value_pack, one_hot, image_pack, mask_pack = pack_inputs(pack_index)
        scores = pack_scores(query_pack, key_pack, expanded, one_hot, image_pack, mask_pack)
        log_total = log_norm(scores)
        attn_probs = jnp.exp(scores - log_total)
        norm_list.append(log_total)
        pack_out = jnp.einsum(
            "hqk,khd->qhd",
            attn_probs.astype(jnp.bfloat16),
            value_pack,
            preferred_element_type=jnp.float32,
        )
        head_list.append(pack_out.reshape(LONG, local_width).astype(jnp.bfloat16))
    head_out = jnp.concatenate(head_list, axis=0)
    attn_part = jnp.dot(head_out, w_proj, preferred_element_type=jnp.float32)
    attn_full = lax.psum(attn_part, "narrow") + proj_bias.astype(jnp.float32)
    middle = inputs + scales[0] * attn_full
    normed_two, unit_two, inverse_two = normalize(middle, gains[1], shifts[1])
    normed_two_low = normed_two.astype(jnp.bfloat16)
    hidden = jnp.dot(normed_two_low, w_fc1, preferred_element_type=jnp.float32) + fc1_bias.astype(
        jnp.float32
    )
    active, gelu_back = jax.vjp(partial(jax.nn.gelu, approximate=False), hidden)
    active_low = active.astype(jnp.bfloat16)
    mlp_part = jnp.dot(active_low, w_fc2, preferred_element_type=jnp.float32)
    mixed_out = lax.psum(mlp_part, "narrow") + fc2_bias.astype(jnp.float32)
    block_out = (middle + scales[1] * mixed_out).astype(jnp.bfloat16)
    upstream = d_out.astype(jnp.float32)
    grad_mixed = (scales[1] * upstream).astype(jnp.bfloat16)
    d_scale_two = jnp.sum(upstream * mixed_out, axis=0)
    d_fc2 = jnp.einsum("rf,rd->fd", active_low, grad_mixed, preferred_element_type=jnp.float32)
    d_fc2_bias = jnp.sum(grad_mixed.astype(jnp.float32), axis=0)
    grad_active = jnp.einsum("rd,fd->rf", grad_mixed, w_fc2, preferred_element_type=jnp.float32)
    grad_hidden = gelu_back(grad_active)[0].astype(jnp.bfloat16)
    d_fc1 = jnp.einsum("rd,rf->df", normed_two_low, grad_hidden, preferred_element_type=jnp.float32)
    d_fc1_bias = jnp.sum(grad_hidden.astype(jnp.float32), axis=0)
    grad_normed_two = lax.psum(
        jnp.einsum("rf,df->rd", grad_hidden, w_fc1, preferred_element_type=jnp.float32), "narrow"
    )
    middle_part, d_gain_two, d_shift_two = normalize_back(
        grad_normed_two, unit_two, inverse_two, gains[1]
    )
    grad_middle = upstream + middle_part
    grad_branch = (scales[0] * grad_middle).astype(jnp.bfloat16)
    d_scale_one = jnp.sum(grad_middle * attn_full, axis=0)
    d_proj = jnp.einsum("rc,rd->cd", head_out, grad_branch, preferred_element_type=jnp.float32)
    d_proj_bias = jnp.sum(grad_branch.astype(jnp.float32), axis=0)
    grad_heads = jnp.einsum(
        "rd,cd->rc", grad_branch, w_proj, preferred_element_type=jnp.float32
    ).astype(jnp.bfloat16)
    table_grad = jnp.zeros((local_heads, padded, padded), jnp.float32)
    query_grads = []
    key_grads = []
    value_grads = []
    for pack_index in range(pack_count):
        query_pack, key_pack, value_pack, one_hot, image_pack, mask_pack = pack_inputs(pack_index)
        scores = pack_scores(query_pack, key_pack, expanded, one_hot, image_pack, mask_pack)
        attn_probs = jnp.exp(scores - norm_list[pack_index])
        grad_pack = grad_heads[pack_index * LONG : (pack_index + 1) * LONG].reshape(pack_shape)
        grad_probs = jnp.einsum(
            "qhd,khd->hqk", grad_pack, value_pack, preferred_element_type=jnp.float32
        )
        row_inner = jnp.sum(attn_probs * grad_probs, axis=-1, keepdims=True)
        grad_scores = (attn_probs * (grad_probs - row_inner)).astype(jnp.bfloat16)
        grad_query = (
            jnp.einsum(
                "hqk,khd->qhd", grad_scores, key_pack, preferred_element_type=jnp.float32
            ).astype(jnp.bfloat16)
            * head_scale
        )
        grad_key = jnp.einsum(
            "hqk,qhd->khd", grad_scores, query_pack, preferred_element_type=jnp.float32
        ).astype(jnp.bfloat16)
        grad_value = jnp.einsum(
            "hqk,qhd->khd",
            attn_probs.astype(jnp.bfloat16),
            grad_pack,
            preferred_element_type=jnp.float32,
        ).astype(jnp.bfloat16)
        query_grads.append(grad_query.reshape(LONG, local_width))
        key_grads.append(grad_key.reshape(LONG, local_width))
        value_grads.append(grad_value.reshape(LONG, local_width))
        by_key = jnp.einsum("hqk,kc->hqc", grad_scores, one_hot, preferred_element_type=jnp.float32)
        upper_part = by_key.astype(jnp.bfloat16)
        lower_part = (by_key - upper_part.astype(jnp.float32)).astype(jnp.bfloat16)
        table_grad = table_grad + jnp.einsum(
            "qc,hqe->hce", one_hot, upper_part, preferred_element_type=jnp.float32
        )
        table_grad = table_grad + jnp.einsum(
            "qc,hqe->hce", one_hot, lower_part, preferred_element_type=jnp.float32
        )
    grad_qkv = jnp.stack(
        [
            jnp.concatenate(query_grads, axis=0),
            jnp.concatenate(key_grads, axis=0),
            jnp.concatenate(value_grads, axis=0),
        ],
        axis=0,
    )
    d_rel_table = table_back(table_grad)
    d_qkv = jnp.einsum("rd,kre->kde", normed_low, grad_qkv, preferred_element_type=jnp.float32)
    d_qv_bias = jnp.stack(
        [
            jnp.sum(grad_qkv[0].astype(jnp.float32), axis=0),
            jnp.sum(grad_qkv[2].astype(jnp.float32), axis=0),
        ],
        axis=0,
    )
    grad_normed_one = lax.psum(
        jnp.einsum("kre,kde->rd", grad_qkv, w_qkv, preferred_element_type=jnp.float32), "narrow"
    )
    input_part, d_gain_one, d_shift_one = normalize_back(
        grad_normed_one, unit_one, inverse_one, gains[0]
    )
    d_tokens = grad_middle + input_part
    (
        d_qkv,
        d_qv_bias,
        d_proj,
        d_proj_bias,
        d_gain_one,
        d_shift_one,
        d_scale_one,
        d_rel_table,
        d_fc1,
        d_fc1_bias,
        d_fc2,
        d_fc2_bias,
        d_gain_two,
        d_shift_two,
        d_scale_two,
    ) = lax.psum(
        (
            d_qkv,
            d_qv_bias,
            d_proj,
            d_proj_bias,
            d_gain_one,
            d_shift_one,
            d_scale_one,
            d_rel_table,
            d_fc1,
            d_fc1_bias,
            d_fc2,
            d_fc2_bias,
            d_gain_two,
            d_shift_two,
            d_scale_two,
        ),
        "wide",
    )
    d_norm_gains = jnp.stack([d_gain_one, d_gain_two], axis=0)
    d_norm_shifts = jnp.stack([d_shift_one, d_shift_two], axis=0)
    d_layer_scales = jnp.stack([d_scale_one, d_scale_two], axis=0)
    return (
        block_out,
        d_tokens,
        d_qkv,
        d_qv_bias,
        d_proj,
        d_proj_bias,
        d_fc1,
        d_fc1_bias,
        d_fc2,
        d_fc2_bias,
        d_norm_gains,
        d_norm_shifts,
        d_layer_scales,
        d_rel_table,
    )


def solution(mesh):
    in_specs = (
        P("wide", None),
        P(None, None, "narrow"),
        P(None, "narrow"),
        P("narrow", None),
        P(),
        P(None, "narrow"),
        P("narrow"),
        P("narrow", None),
        P(),
        P(),
        P(),
        P(),
        P("narrow", None),
        P("wide"),
        P("wide"),
        P("wide"),
        P("wide"),
        P("wide", None),
    )
    out_specs = (
        P("wide", None),
        P("wide", None),
        P(None, None, "narrow"),
        P(None, "narrow"),
        P("narrow", None),
        P(),
        P(None, "narrow"),
        P("narrow"),
        P("narrow", None),
        P(),
        P(),
        P(),
        P(),
        P("narrow", None),
    )
    return jax.shard_map(
        on_device, mesh=mesh, in_specs=in_specs, out_specs=out_specs, check_vma=False
    )
```

profile of v0, /device:TPU:0, one launch (start us, length us, event | category | flops | bytes accessed | tf_op | source)
XLA Modules:
  0.0 683.8 jit_solution(13120151210782741174)
XLA Ops:
  7.3 0.9 slice_convert_fusion
  9.6 1.4 slice_compare_fusion.1
  13.7 1.8 convert_reduce_fusion
  15.5 2.2 fusion.13
  18.6 2.6 fusion.107
  23.1 0.8 fusion.115
  23.9 11.3 %convolution_bitcast_fusion = f32[3,24,24,24,24]{4,3,2,1,0:T(8,128)} fusion(bf16[24,24,47,1,1]{2,1,0,4,3:T(8,128)(2,1)} %constant.110, bf16[24,24,47,1]{2,1,0,3:T(8,128)(2,1)} %constant.109, bf16[3,47,47,1]{2,1,0,3:T(8,128)(2,1)S(1)} %reshape.277), kind=kOutput, calls=%fused_computation | convolution fusion | flops 101276352 | bytes 4102854 | tf_op jit(solution)/shard_map/hrsc,abc->hrasb/dot_general | solution.py:63
  35.2 14.8 %reshape.260 = f32[3,576,576]{2,1,0:T(8,128)} reshape(f32[3,24,24,24,24]{4,3,2,1,0:T(8,128)} %convolution_bitcast_fusion) | data formatting | bytes 7962624 | tf_op jit(solution)/shard_map/reshape | solution.py:64
  50.0 6.3 add_convert_fusion
  56.3 7.7 %fusion.26 = f32[3,584,584]{1,2,0:T(8,128)} fusion(bf16[3,640,640]{2,1,0:T(8,128)(2,1)} %add_convert_fusion, s32[584]{0:T(1024)S(1)} %get-tuple-element.74), kind=kOutput, calls=%fused_computation.74 | convolution fusion | flops 2746762240 | bytes 6552608 | tf_op jit(solution)/shard_map/hqe,ke->hqk/dot_general | solution.py:97
  64.0 1.5 compare_and_fusion
  65.6 3.4 fusion.119
  69.0 2.0 copy-done.2
  71.6 7.7 %fusion.28 = f32[3,584,584]{1,2,0:T(8,128)} fusion(bf16[3,640,640]{2,1,0:T(8,128)(2,1)} %add_convert_fusion, s32[584]{0:T(1024)S(1)} %copy-done.47), kind=kOutput, calls=%fused_computation.76 | convolution fusion | flops 2746762240 | bytes 6552608 | tf_op jit(solution)/shard_map/hqe,ke->hqk/dot_general | solution.py:97
  79.4 3.8 fusion.120
  84.4 0.9 convolution_convert_fusion.8
  85.3 0.9 convolution_convert_fusion.9
  86.9 2.6 fusion.99
  90.3 77.9 %all-reduce.9.cloned.1.call-done = f32[1168,768]{1,0:T(8,128)} async-done(((f32[1168,768]{1,0:T(8,128)}), f32[1168,768]{1,0:T(8,128)}) %all-reduce.9.cloned.1.call-update) | async-done | bytes 3588112 | tf_op jit(solution)/shard_map/psum | solution.py:182
  168.2 2.7 fusion.111
  171.7 10.3 %multiply_convert_fusion.3 = (bf16[1168,768]{1,0:T(8,128)(2,1)}, f32[1168,768]{1,0:T(8,128)S(1)}, f32[1168,768]{1,0:T(8,128)S(1)}) fusion(f32[768]{0:T(1024)S(1)} %copy-done.58, bf16[768,768]{1,0:T(8,128)(2,1)S(1)} %copy-done, f32[1168,768]{1,0:T(8,128)S(1)} %get-tuple-element.57, f32[768]{0:T(1024)S(1)} %copy-done.56, f32[768]{0:T(1024)S(1)} %get-tuple-element.89, ...), kind=kOutput, calls=%fused_computation.50 | convolution fusion | flops 1441517568 | bytes 13756544 | tf_op jit(solution)/shard_map/dot_general | solution.py:186
  182.0 3.3 convert_reduce_fusion.2
  185.3 1.2 copy-done.69
  186.5 3.4 fusion.122
  190.0 1.2 copy-done.67
  191.2 4.9 fusion.121
  196.1 69.8 %all-reduce.11.cloned.1.call-done = f32[1168,768]{1,0:T(8,128)} async-done(((f32[1168,768]{1,0:T(8,128)}), f32[1168,768]{1,0:T(8,128)}) %all-reduce.11.cloned.1.call-update) | async-done | bytes 3588112 | tf_op jit(solution)/shard_map/psum | solution.py:203
  265.9 4.7 multiply_reduce_fusion.3
  271.1 3.9 multiply_reduce_fusion.2
  277.8 1.5 slice-done.4
  280.2 1.0 multiply_reduce_fusion.1
  281.3 1.0 multiply_convert_fusion.1
  283.8 0.8 convolution_convert_fusion.2
  284.7 1.0 multiply_reduce_fusion
  285.7 1.0 multiply_convert_fusion
  289.2 3.4 convolution_bitcast_fusion.1
  293.4 5.5 fusion.62
  298.9 3.6 fusion.109
  302.5 1.4 fusion.98
  304.0 4.5 fusion.41
  308.5 2.8 fusion.34
  312.0 4.3 fusion.49
  316.4 2.9 fusion.39
  319.2 2.6 fusion.24
  321.9 2.6 fusion.25
  324.5 5.2 add_bitcast_fusion
  329.7 2.6 slice.174
  332.3 0.8 stack.67
  333.7 0.9 slice_reduce_fusion.1
  334.7 14.5 %reshape.272 = f32[3,24,24,24,24]{2,1,4,3,0:T(8,128)} reshape(f32[3,576,576]{1,2,0:T(8,128)} %slice.174) | data formatting | bytes 7962624 | tf_op jit(solution)/shard_map/reshape | solution.py:80
  349.2 20.5 %fusion.123 = f32[3,24,24,47,1]{3,1,4,2,0:T(8,128)S(1)} fusion(f32[3,24,24,24,24]{2,1,4,3,0:T(8,128)} %reshape.272, f32[24,24,47,1,1]{2,0,1,4,3:T(8,128)} %constant.112), kind=kOutput, calls=%fused_computation.190 | convolution fusion | flops 561364992 | bytes 4414464 | tf_op jit(solution)/shard_map/hrasb,abk->hrsk/dot_general | solution.py:81
  369.7 2.2 convolution_bitcast_fusion.2
  371.9 1.0 copy.60
  373.1 1.2 convert_reduce_fusion.4
  374.6 52.5 %all-reduce.15.cloned.1.call-done = (f32[1168,768]{1,0:T(8,128)}, f32[1168,768]{1,0:T(8,128)}) async-done(((f32[1168,768]{1,0:T(8,128)}, f32[1168,768]{1,0:T(8,128)}), (f32[1168,768]{1,0:T(8,128)}, f32[1168,768]{1,0:T(8,128)})) %all-reduce.15.cloned.1.call-update) | async-done | bytes 7176208 | tf_op jit(solution)/shard_map/psum | solution.py:192
  427.1 6.0 fusion.16
  433.1 2.1 fusion.12
  435.2 42.0 %all-reduce.1 = (f32[2,192]{1,0:T(2,128)}, f32[768]{0:T(1024)}, f32[768]{0:T(1024)}, f32[768]{0:T(1024)}, f32[1,768]{1,0:T(1,128)S(1)}, /*index=5*/f32[1,768]{1,...) all-reduce(f32[2,192]{1,0:T(2,128)S(1)} %pad_maximum_fusion.11, ...), channel_id=1, replica_groups=mesh['wide'=8,'narrow'=4] {'wide'}, use_global_device_ids=true, to_apply=%region_21.22 | all-reduce | flops 13932 | bytes 111456 | tf_op jit(solution)/shard_map/psum | solution.py:298
  479.0 5.1 fusion.11
  484.1 186.2 %all-reduce.13.cloned.1.call-done = (f32[3,768,192]{1,2,0:T(8,128)}, f32[192,768]{1,0:T(8,128)}, f32[768,768]{1,0:T(8,128)}, f32[768,768]{1,0:T(8,128)}) async-done(((f32[3,768,192]{1,2,0:T(8,128)}, f32[192,768]{1,0:T(8,128)}, f32[768,768]{1,0:T(8,128)}, f32[768,768]{1,0:T(8,128)}), (f32[3,768,192]{1,2,0:T(8,128)}, f32[192,768]{1,0:T(8,128)}, f32[768,768]{1,0:T(8,128)}, ...) | async-done | bytes 7077904 | tf_op jit(solution)/shard_map/psum | solution.py:298
  670.3 2.9 copy.95
  673.2 0.8 copy.96
  674.0 1.4 copy.97
  675.5 1.4 copy.98
  (225 shorter events, 23.3 us)
Async XLA Ops:
  7.2 164.4 %copy-start = (bf16[768,768]{1,0:T(8,128)(2,1)S(1)}, bf16[768,768]{1,0:T(8,128)(2,1)}, u32[]{:S(2)}) copy-start(bf16[768,768]{1,0:T(8,128)(2,1)} %param.28) | copy-start | bytes 3538948
  7.2 10.6 %copy-start.44 = (bf16[3,2212]{1,0:T(4,128)(2,1)S(1)}, bf16[3,2212]{1,0:T(4,128)(2,1)}, u32[]{:S(2)}) copy-start(bf16[3,2212]{1,0:T(4,128)(2,1)} %param.35) | copy-start | bytes 39820
  7.2 11.3 %copy-start.7 = (bf16[1168,768]{1,0:T(8,128)(2,1)S(1)}, bf16[1168,768]{1,0:T(8,128)(2,1)}, u32[]{:S(2)}) copy-start(bf16[1168,768]{1,0:T(8,128)(2,1)} %param.23) | copy-start | bytes 5382148
  7.2 10.5 %copy-start.50 = (s32[1168]{0:T(1024)S(1)}, s32[1168]{0:T(1024)}, u32[]{:S(2)}) copy-start(s32[1168]{0:T(1024)} %param.36) | copy-start | bytes 14020
  7.2 161.0 %all-reduce.9.cloned.1.call-start = ((), (), s32[]{:S(2)}) async-start(), calls=%async_computation | async-start | bytes 7176192 | tf_op jit(solution)/shard_map/psum | solution.py:182
  13.7 42.6 %copy-start.45 = (s32[584]{0:T(1024)}, s32[584]{0:T(1024)S(1)}, u32[]{:S(2)}) copy-start(s32[584]{0:T(1024)S(1)} %get-tuple-element.74) | copy-start | bytes 7012
  18.6 2.6 copy-start.53
  35.2 14.8 %copy-start.60 = (f32[3]{0:T(128)S(1)}, f32[3]{0:T(128)}, u32[]{:S(2)}) copy-start(f32[3]{0:T(128)} %get-tuple-element.30) | copy-start | bytes 40
  35.2 14.8 %copy-start.61 = (f32[3]{0:T(128)S(1)}, f32[3]{0:T(128)}, u32[]{:S(2)}) copy-start(f32[3]{0:T(128)} %get-tuple-element.31) | copy-start | bytes 40
  35.2 14.8 %copy-start.62 = (f32[3]{0:T(128)S(1)}, f32[3]{0:T(128)}, u32[]{:S(2)}) copy-start(f32[3]{0:T(128)} %get-tuple-element.32) | copy-start | bytes 40
  56.3 7.7 %copy-start.51 = (pred[584]{0:T(1024)(128)(4,1)S(1)}, pred[584]{0:T(1024)(128)(4,1)}, u32[]{:S(2)}) copy-start(pred[584]{0:T(1024)(128)(4,1)} %get-tuple-element.69) | copy-start | bytes 1756
  56.3 7.7 %copy-start.52 = (pred[584]{0:T(1024)(128)(4,1)S(1)}, pred[584]{0:T(1024)(128)(4,1)}, u32[]{:S(2)}) copy-start(pred[584]{0:T(1024)(128)(4,1)} %get-tuple-element.70) | copy-start | bytes 1756
  68.9 2.0 copy-start.2
  68.9 2.7 copy-start.47
  79.4 4.5 slice-start
  79.4 4.5 slice-start.1
  83.2 2.1 copy-start.3
  86.9 2.7 copy-start.63
  86.9 2.7 copy-start.64
  86.9 3.4 copy-start.59
  89.6 176.3 %all-reduce.11.cloned.1.call-start = ((), (), s32[]{:S(2)}) async-start(), calls=%async_computation.1 | async-start | bytes 7176192 | tf_op jit(solution)/shard_map/psum | solution.py:203
  170.9 11.0 %copy-start.4 = (f32[1168,768]{1,0:T(8,128)}, f32[1168,768]{1,0:T(8,128)S(1)}, u32[]{:S(2)}) copy-start(f32[1168,768]{1,0:T(8,128)S(1)} %get-tuple-element.57) | copy-start | bytes 10764292
  171.7 10.3 %copy-start.15 = (bf16[1168,768]{1,0:T(8,128)(2,1)S(1)}, bf16[1168,768]{1,0:T(8,128)(2,1)}, u32[]{:S(2)}) copy-start(bf16[1168,768]{1,0:T(8,128)(2,1)} %param.40) | copy-start | bytes 5382148
  171.7 10.3 %copy-start.66 = (bf16[768,768]{1,0:T(8,128)(2,1)S(1)}, bf16[768,768]{1,0:T(8,128)(2,1)}, u32[]{:S(2)}) copy-start(bf16[768,768]{1,0:T(8,128)(2,1)} %param.30) | copy-start | bytes 3538948
  189.9 237.1 %all-reduce.15.cloned.1.call-start = ((), (), s32[]{:S(2)}) async-start(), calls=%async_computation.3 | async-start | bytes 14352384 | tf_op jit(solution)/shard_map/psum | solution.py:192
  265.9 4.7 copy-start.5
  265.9 5.2 copy-start.13
  275.1 4.2 slice-start.4
  275.1 4.2 slice-start.5
  275.7 2.2 copy-start.28
  277.0 3.1 copy-start.24
  280.2 7.9 %copy-start.25 = (bf16[3,64,584]{2,1,0:T(8,128)(2,1)}, bf16[3,64,584]{2,1,0:T(8,128)(2,1)S(1)}, u32[]{:S(2)}) copy-start(bf16[3,64,584]{2,1,0:T(8,128)(2,1)S(1)} %convolution_convert_fusion.3) | copy-start | bytes 672772
  280.2 3.6 slice-start.2
  281.3 2.6 slice-start.3
  282.5 2.2 copy-start.11
  284.7 3.4 copy-start.27
  286.8 2.5 copy-start.68
  289.2 3.4 copy-start.39
  292.7 377.6 %all-reduce.13.cloned.1.call-start = ((), (), s32[]{:S(2)}) async-start(), calls=%async_computation.2 | async-start | bytes 14155776 | tf_op jit(solution)/shard_map/psum | solution.py:298
  293.4 5.5 copy-start.6
  293.4 5.5 copy-start.57
  293.4 5.5 copy-start.70
  298.9 3.7 copy-start.29
  298.9 3.7 copy-start.31
  298.9 3.7 copy-start.33
  298.9 5.0 copy-start.12
  298.9 5.0 copy-start.48
  303.9 4.6 copy-start.36
  303.9 4.6 copy-start.38
  303.9 4.6 copy-start.40
  304.0 4.5 copy-start.54
  311.3 5.0 slice-start.6
  312.0 4.3 slice-start.7
  316.4 5.5 copy-start.16
  329.6 3.6 copy-start.9
  349.2 20.5 %copy-start.43 = (f32[24,24,47,1]{2,1,0,3:T(8,128)S(1)}, f32[24,24,47,1]{2,1,0,3:T(8,128)}, u32[]{:S(2)}) copy-start(f32[24,24,47,1]{2,1,0,3:T(8,128)} %constant.113) | copy-start | bytes 324868
  349.2 23.9 %copy-start.26 = (bf16[3,64,584]{2,1,0:T(8,128)(2,1)S(1)}, bf16[3,64,584]{2,1,0:T(8,128)(2,1)}, u32[]{:S(2)}) copy-start(bf16[3,64,584]{2,1,0:T(8,128)(2,1)} %copy-done.25) | copy-start | bytes 672772
  427.1 6.0 copy-start.14
  433.0 2.1 copy-start.49
  433.0 2.1 copy-start.55
  670.3 3.0 copy-start.34
  670.3 3.8 copy-start.18
  673.2 2.2 copy-start.17
  673.2 3.6 copy-start.1
  (19 other events, 22.3 us)
Sparse Core Ops, SparseCore 0:
  89.7 78.4 all-reduce.8
  190.1 75.8 all-reduce.10
  292.8 134.1 all-reduce.14
  432.5 237.7 all-reduce.12
where the time goes:
time: 693 us; the launch traced here: 684 us
  waiting for transfers between devices  386 us (56%)
  matrix products  131 us (19%)
  local copies, waits for them, and re-layouts  57.4 us (8%)
  other arithmetic  51.1 us (7%)
  blocking collectives  42 us (6%)
  between operations  15.2 us (2%)
    psum x1, waiting for transfers between devices, on_device(): lax.psum((d_qkv, d_qv_bias, d_proj, d_proj_bias, d_gain_one, d_shift_one,...  186 us
    psum x1, waiting for transfers between devices, on_device(): attn_full = lax.psum(attn_part, 'narrow') + proj_bias.astype(jnp.float32)  77.9 us
    psum x1, waiting for transfers between devices, on_device(): lax.psum(jnp.einsum('rf,df->rd', grad_hidden, w_fc1, preferred_element_ty...  69.8 us
    psum x1, waiting for transfers between devices, on_device(): mixed_out = lax.psum(mlp_part, 'narrow') + fc2_bias.astype(jnp.float32)  52.5 us
    psum x1, blocking collectives, on_device(): lax.psum((d_qkv, d_qv_bias, d_proj, d_proj_bias, d_gain_one, d_shift_one,...  42 us
    dot_general x1, matrix products, table_back(): jnp.einsum('hrasb,abk->hrsk', patch_grad, shift_full, precision=lax.Preci...  20.5 us
    unnamed x163, local copies, waits for them, and re-layouts  17.8 us
    dot_general x2, matrix products, pack_scores(): jnp.einsum('hqe,ke->hqk', by_query, one_hot, preferred_element_type=jnp.f...  15.4 us
  transfers between devices with their start and end apart: 4, of which 4 were waited for; matrix products, arithmetic and copies ran while one was open for 15% of the time, Pallas kernels for 0%

commit v1 on v0

v1 whole, which is shorter than its diff:
```python
from functools import partial

import jax
import jax.numpy as jnp
import numpy as np
from jax import lax
from jax.experimental import pallas as pl
from jax.experimental.pallas import tpu as pltpu
from jax.sharding import PartitionSpec as P

HD = 64
GRID = 24
SMALL = 14
SHORT = 208
LONG = 584
EPSILON = 1e-06
SIDE = 2 * GRID - 1
WIDE_L = 1280
WIDE_S = 640
NEG = -1e30
F32 = jnp.float32
BF16 = jnp.bfloat16
VMEM_LIMIT = 56 << 20


def params(**kw):
    return pltpu.CompilerParams(vmem_limit_bytes=VMEM_LIMIT, **kw)


def dot(a, b):
    return jnp.dot(a, b, preferred_element_type=F32)


def dot_nt(a, b):
    return lax.dot_general(a, b, (((1,), (1,)), ((), ())), preferred_element_type=F32)


def dot_tn(a, b):
    return lax.dot_general(a, b, (((0,), (0,)), ((), ())), preferred_element_type=F32)


def large_pick():
    pick = np.zeros((2, SIDE, GRID, GRID), np.float32)
    for s in range(GRID):
        for c in range(GRID):
            if s == 0:
                pick[1, c, s, c] = 1
            else:
                pick[0, c + GRID - s, s, c] = 1
    return pick.reshape(2 * SIDE, GRID * GRID)


def small_pick():
    pick = np.zeros((SIDE, 16, SMALL), np.float32)
    for s in range(SMALL):
        for c in range(SMALL):
            pick[c - s + GRID - 1, s, c] = 1
    return pick.reshape(SIDE, 16 * SMALL)


def strips(rel_table):
    heads = rel_table.shape[0]
    grid_part = rel_table[:, : SIDE * SIDE].reshape(heads, SIDE, SIDE)
    front = jnp.pad(grid_part, ((0, 0), (1, 0), (0, 0)))
    back = jnp.pad(grid_part, ((0, 0), (0, 1), (0, 0)))
    both = jnp.concatenate([front, back], axis=2)
    large = jnp.einsum(
        "huk,kp->hup", both, jnp.asarray(large_pick(), BF16), preferred_element_type=F32
    ).reshape(heads, SIDE + 1, GRID, GRID)
    large = large.transpose(0, 2, 1, 3).reshape(heads, GRID, (SIDE + 1) * GRID)
    large = jnp.pad(large, ((0, 0), (0, 0), (1, WIDE_L - 1 - (SIDE + 1) * GRID)))
    rows = 2 * SMALL - 1
    part = grid_part[:, GRID - SMALL : GRID - SMALL + rows]
    small = jnp.einsum(
        "huk,kp->hup", part, jnp.asarray(small_pick(), BF16), preferred_element_type=F32
    ).reshape(heads, rows, 16, SMALL)
    small = small.transpose(0, 2, 1, 3).reshape(heads, 16, rows * SMALL)
    small = jnp.pad(small, ((0, 0), (0, 0), (1, WIDE_S - 1 - rows * SMALL)))
    tails = rel_table[:, SIDE * SIDE :].astype(F32)
    return large, small, tails


def strips_back(d_large, d_small, d_tails):
    heads = d_large.shape[0]
    rows = 2 * SMALL - 1
    hi = lax.Precision.HIGHEST
    large = d_large[:, :, 1 : 1 + (SIDE + 1) * GRID].reshape(heads, GRID, SIDE + 1, GRID)
    both = jnp.einsum(
        "hsuc,ksc->huk",
        large,
        jnp.asarray(large_pick().reshape(2 * SIDE, GRID, GRID)),
        precision=hi,
    )
    grid_grad = both[:, 1:, :SIDE] + both[:, :SIDE, SIDE:]
    small = d_small[:, :, 1 : 1 + rows * SMALL].reshape(heads, 16, rows, SMALL)
    part = jnp.einsum(
        "hsuc,ksc->huk", small, jnp.asarray(small_pick().reshape(SIDE, 16, SMALL)), precision=hi
    )
    low = GRID - SMALL
    grid_grad = grid_grad + jnp.pad(part, ((0, 0), (low, SIDE - low - rows), (0, 0)))
    return jnp.concatenate(
        [grid_grad.reshape(heads, SIDE * SIDE), d_tails[:, 0, :3]], axis=1
    )


def tail_fix(block, t0, t1, t2, last, real):
    shape = block.shape
    row = lax.broadcasted_iota(jnp.int32, shape, 0)
    lane = lax.broadcasted_iota(jnp.int32, shape, 1)
    block = jnp.where(lane > last, block[:, 1:2], block)
    block = jnp.where(lane == 0, t0, block)
    block = jnp.where(row == 0, jnp.where(lane == 0, t2, t1), block)
    return jnp.where(row >= real, NEG, block)


def bias_kernel(tail_ref, large_ref, small_ref, out_ref, scr):
    for h in range(large_ref.shape[0]):
        t0, t1, t2 = tail_ref[h, 0], tail_ref[h, 1], tail_ref[h, 2]
        for r in range(GRID + 1):
            size = GRID if r < GRID else LONG - GRID * GRID
            off = (GRID - r) * GRID
            scr[r * GRID : r * GRID + size, 0:LONG] = large_ref[h, 0:size, off : off + LONG]
        last = GRID * GRID
        out_ref[0, h] = tail_fix(scr[:, 0:LONG], t0, t1, t2, last, last + 1).astype(BF16)
        last = SMALL * SMALL
        for r in range(SMALL):
            off = (SMALL - 1 - r) * SMALL
            wide = LONG - SHORT
            scr[1 + r * SMALL : 1 + (r + 1) * SMALL, 0:wide] = small_ref[
                h, 0:SMALL, off : off + wide
            ]
        block = tail_fix(scr[0:SHORT, 0 : LONG - SHORT], t0, t1, t2, last, last + 1)
        scr[...] = jnp.full(scr.shape, NEG, F32)
        scr[0:SHORT, 0:SHORT] = block[:, 0:SHORT]
        scr[SHORT : 2 * SHORT, SHORT:LONG] = block
        out_ref[1, h] = scr[:, 0:LONG].astype(BF16)


def make_bias(rel_table):
    heads = rel_table.shape[0]
    large, small, tails = strips(rel_table)
    return pl.pallas_call(
        bias_kernel,
        out_shape=jax.ShapeDtypeStruct((2, heads, LONG, LONG), BF16),
        in_specs=[
            pl.BlockSpec(memory_space=pltpu.SMEM),
            pl.BlockSpec(memory_space=pltpu.VMEM),
            pl.BlockSpec(memory_space=pltpu.VMEM),
        ],
        out_specs=pl.BlockSpec(memory_space=pltpu.VMEM),
        scratch_shapes=[pltpu.VMEM((LONG, 640), F32)],
        compiler_params=params(),
        name="bias",
    )(tails, large, small)


def layer_norm(values, gain_row, shift_row):
    row_mean = jnp.mean(values, axis=-1, keepdims=True)
    centred = values - row_mean
    inverse = lax.rsqrt(jnp.mean(centred * centred, axis=-1, keepdims=True) + EPSILON)
    unit_rows = centred * inverse
    return unit_rows * gain_row + shift_row, unit_rows, inverse


def head_lanes(shape, h):
    lane = lax.broadcasted_iota(jnp.int32, shape, 1)
    return (lane >= h * HD) & (lane < (h + 1) * HD)


def turned(block):
    return block.astype(F32).T.astype(BF16)


def forward_kernel(
    sc_ref, tok_ref, w_ref, qv_ref, gain_ref, shift_ref, bias_ref, o_ref, q_ref, k_ref, v_ref, lse_ref
):
    x = tok_ref[0].astype(F32)
    n1 = layer_norm(x, gain_ref[...], shift_ref[...])[0].astype(BF16)
    q = ((dot(n1, w_ref[0]) + qv_ref[0:1]) * HD**-0.5).astype(BF16)
    k = dot(n1, w_ref[1]).astype(BF16)
    v = (dot(n1, w_ref[2]) + qv_ref[1:2]).astype(BF16)
    q_ref[0] = q
    k_ref[0] = k
    v_ref[0] = v
    v_t = turned(v)
    outs = []
    for h in range(k.shape[1] // HD):
        k_h = jnp.where(head_lanes(k.shape, h), k, jnp.zeros_like(k))
        s = dot_nt(k_h, q) + bias_ref[0, h].astype(F32)
        top = jnp.max(s, axis=0, keepdims=True)
        e = jnp.exp(s - top)
        total = jnp.sum(e, axis=0, keepdims=True)
        p = (e * (1.0 / total)).astype(BF16)
        outs.append(dot(v_t[h * HD : (h + 1) * HD], p))
        lse_ref[0, h : h + 1, :] = top + jnp.log(total)
    o_ref[0] = jnp.concatenate(outs, axis=0).T.astype(BF16).astype(F32)


def pack_spec(shape):
    return pl.BlockSpec((1,) + shape, lambda i, sc: (sc[0],) + (0,) * len(shape))


def first_spec(shape):
    return pl.BlockSpec((1,) + shape, lambda i, sc: (0,) * (1 + len(shape)))


def whole_spec(shape):
    return pl.BlockSpec(shape, lambda i, sc: (0,) * len(shape))


def kind_spec(shape):
    return pl.BlockSpec((1,) + shape, lambda i, sc: (sc[1],) + (0,) * len(shape))


def attend(scalars, tok3, w_qkv, qv_bias, gain_row, shift_row, bias):
    width = w_qkv.shape[2]
    heads = width // HD
    dim = tok3.shape[2]
    low = jax.ShapeDtypeStruct((1, LONG, width), BF16)
    return pl.pallas_call(
        forward_kernel,
        out_shape=[
            jax.ShapeDtypeStruct((1, LONG, width), F32),
            low,
            low,
            low,
            jax.ShapeDtypeStruct((1, heads, LONG), F32),
        ],
        grid_spec=pltpu.PrefetchScalarGridSpec(
            num_scalar_prefetch=1,
            grid=(1,),
            in_specs=[
                pack_spec((LONG, dim)),
                whole_spec((3, dim, width)),
                whole_spec((2, width)),
                whole_spec((1, dim)),
                whole_spec((1, dim)),
                kind_spec((heads, LONG, LONG)),
            ],
            out_specs=[first_spec((LONG, width))] * 4 + [first_spec((heads, LONG))],
        ),
        compiler_params=params(),
        cost_estimate=pl.CostEstimate(
            flops=2 * LONG * dim * 3 * width + 4 * LONG * LONG * width,
            transcendentals=heads * LONG * LONG,
            bytes_accessed=2 * heads * LONG * LONG + 8 * LONG * dim,
        ),
        name="attend",
    )(scalars, tok3, w_qkv, qv_bias, gain_row, shift_row, bias)


def fold_large(ds, h, dl_ref, dt_ref):
    last = GRID * GRID
    full = ds[:, 0:LONG]
    lane = lax.broadcasted_iota(jnp.int32, full.shape, 1)
    row = lax.broadcasted_iota(jnp.int32, full.shape, 0)
    pad = jnp.sum(jnp.where(lane > last, full, 0.0), axis=1, keepdims=True)
    body = row > 0
    t0 = jnp.sum(jnp.where((lane == 0) & body, full, 0.0))
    t1 = jnp.sum(jnp.where((lane > 0) & (row == 0), full, 0.0))
    t2 = jnp.sum(jnp.where((lane == 0) & (row == 0), full, 0.0))
    full = jnp.where((lane == 0) | (lane > last), 0.0, full)
    full = jnp.where(lane == 1, full + pad, full)
    ds[:, 0:LONG] = jnp.where(body, full, 0.0)
    for r in range(GRID + 1):
        size = GRID if r < GRID else LONG - GRID * GRID
        off = (GRID - r) * GRID
        dl_ref[h, 0:size, off : off + LONG] += ds[r * GRID : r * GRID + size, 0:LONG]
    tail_add(dt_ref, h, t0, t1, t2)


def tail_add(dt_ref, h, t0, t1, t2):
    lane = lax.broadcasted_iota(jnp.int32, (8, 128), 1)
    row = lax.broadcasted_iota(jnp.int32, (8, 128), 0)
    add = jnp.where(lane == 0, t0, jnp.where(lane == 1, t1, jnp.where(lane == 2, t2, 0.0)))
    dt_ref[h] += jnp.where(row == 0, add, 0.0)


def fold_small(ds, h, ds_ref, dt_ref):
    last = SMALL * SMALL
    for base, wide in ((0, SHORT), (SHORT, LONG - SHORT)):
        full = ds[base : base + SHORT, 0:LONG]
        if base:
            full = full[:, base : base + wide]
        else:
            full = full[:, 0:wide]
        lane = lax.broadcasted_iota(jnp.int32, full.shape, 1)
        row = lax.broadcasted_iota(jnp.int32, full.shape, 0)
        pad = jnp.sum(jnp.where(lane > last, full, 0.0), axis=1, keepdims=True)
        body = row > 0
        t0 = jnp.sum(jnp.where((lane == 0) & body, full, 0.0))
        t1 = jnp.sum(jnp.where((lane > 0) & (row == 0), full, 0.0))
        t2 = jnp.sum(jnp.where((lane == 0) & (row == 0), full, 0.0))
        full = jnp.where((lane == 0) | (lane > last), 0.0, full)
        full = jnp.where(lane == 1, full + pad, full)
        ds[base : base + SHORT, 0:wide] = full
        for r in range(SMALL):
            off = (SMALL - 1 - r) * SMALL
            lo = base + 1 + r * SMALL
            ds_ref[h, 0:SMALL, off : off + wide] += ds[lo : lo + SMALL, 0:wide]
        tail_add(dt_ref, h, t0, t1, t2)


def backward_kernel(
    sc_ref,
    tok_ref,
    w_ref,
    gain_ref,
    shift_ref,
    bias_ref,
    q_ref,
    k_ref,
    v_ref,
    do_ref,
    lse_ref,
    aw_ref,
    ab_ref,
    al_ref,
    as_ref,
    at_ref,
    dn_ref,
    dw_ref,
    db_ref,
    dl_ref,
    ds_ref,
    dt_ref,
    scr,
):
    dl_ref[...] = al_ref[...]
    ds_ref[...] = as_ref[...]
    dt_ref[...] = at_ref[...]
    q, k, v = q_ref[0], k_ref[0], v_ref[0]
    do = do_ref[0].astype(BF16)
    k_t = turned(k)
    d_qt = []
    d_k = jnp.zeros(k.shape, F32)
    d_v = jnp.zeros(k.shape, F32)
    for h in range(k.shape[1] // HD):
        own = head_lanes(k.shape, h)
        s = dot_nt(jnp.where(own, k, jnp.zeros_like(k)), q) + bias_ref[0, h].astype(F32)
        p = jnp.exp(s - lse_ref[0, h : h + 1, :])
        dp = dot_nt(jnp.where(own, v, jnp.zeros_like(v)), do)
        inner = jnp.sum(p * dp, axis=0, keepdims=True)
        ds = (p * (dp - inner)).astype(BF16)
        d_v = jnp.where(own, dot(p.astype(BF16), do), d_v)
        d_k = jnp.where(own, dot(ds, q), d_k)
        d_qt.append(dot(k_t[h * HD : (h + 1) * HD], ds))
        scr[:, 0:LONG] = ds.astype(F32)

        @pl.when(sc_ref[1] == 0)
        def _():
            fold_large(scr, h, dl_ref, dt_ref)

        @pl.when(sc_ref[1] == 1)
        def _():
            fold_small(scr, h, ds_ref, dt_ref)

    d_q = jnp.concatenate(d_qt, axis=0).T.astype(BF16) * jnp.asarray(HD**-0.5, BF16)
    d_k = d_k.astype(BF16)
    d_v = d_v.astype(BF16)
    dn = dot_nt(d_q, w_ref[0]) + dot_nt(d_k, w_ref[1]) + dot_nt(d_v, w_ref[2])
    half = dn.shape[1] // 2
    dn_ref[0] = dn[:, :half]
    dn_ref[1] = dn[:, half:]
    x = tok_ref[0].astype(F32)
    n1_t = layer_norm(x, gain_ref[...], shift_ref[...])[0].T.astype(BF16)
    dw_ref[0] = aw_ref[0] + dot(n1_t, d_q)
    dw_ref[1] = aw_ref[1] + dot(n1_t, d_k)
    dw_ref[2] = aw_ref[2] + dot(n1_t, d_v)
    db_ref[0:1] = ab_ref[0:1] + jnp.sum(d_q.astype(F32), axis=0, keepdims=True)
    db_ref[1:2] = ab_ref[1:2] + jnp.sum(d_v.astype(F32), axis=0, keepdims=True)


def attend_back(scalars, tok3, w_qkv, gain_row, shift_row, bias, saved, do, sums):
    width = w_qkv.shape[2]
    heads = width // HD
    dim = tok3.shape[2]
    q, k, v, lse = saved
    sum_shapes = [s.shape for s in sums]
    return pl.pallas_call(
        backward_kernel,
        out_shape=[jax.ShapeDtypeStruct((2, LONG, dim // 2), F32)]
        + [jax.ShapeDtypeStruct(s, F32) for s in sum_shapes],
        grid_spec=pltpu.PrefetchScalarGridSpec(
            num_scalar_prefetch=1,
            grid=(1,),
            in_specs=[
                pack_spec((LONG, dim)),
                whole_spec((3, dim, width)),
                whole_spec((1, dim)),
                whole_spec((1, dim)),
                kind_spec((heads, LONG, LONG)),
                first_spec((LONG, width)),
                first_spec((LONG, width)),
                first_spec((LONG, width)),
                first_spec((LONG, width)),
                first_spec((heads, LONG)),
            ]
            + [whole_spec(s) for s in sum_shapes],
            out_specs=[whole_spec((2, LONG, dim // 2))] + [whole_spec(s) for s in sum_shapes],
            scratch_shapes=[pltpu.VMEM((LONG, 640), F32)],
        ),
        compiler_params=params(),
        cost_estimate=pl.CostEstimate(
            flops=4 * LONG * dim * 3 * width + 10 * LONG * LONG * width,
            transcendentals=heads * LONG * LONG,
            bytes_accessed=2 * heads * LONG * LONG + 16 * LONG * dim,
        ),
        name="attend_back",
    )(scalars, tok3, w_qkv, gain_row, shift_row, bias, q, k, v, do, lse, *sums)


def zero_sums(heads, dim, width):
    return [
        jnp.zeros((3, dim, width), F32),
        jnp.zeros((2, width), F32),
        jnp.zeros((heads, GRID, WIDE_L), F32),
        jnp.zeros((heads, 16, WIDE_S), F32),
        jnp.zeros((heads, 8, 128), F32),
    ]


def wide_rows(lo_ref, hi_ref):
    return jnp.concatenate([lo_ref[0], hi_ref[0]], axis=1)


def column_sum(x):
    return jnp.sum(x, axis=0, keepdims=True)


def feed_kernel(first, *refs):
    (sc_ref, tok_ref, out_ref, o0, ox, oc, wp0, wpx, wpc, pb, ls, gain, shift, w1, b1, w2) = refs[:16]
    refs = refs[16:]
    if not first:
        a1, a2, ab1, ab2 = refs[:4]
        refs = refs[4:]
    mid_ref, a_ref, m_ref, dn_ref, d1_ref, d2_ref, db1_ref, db2_ref = refs
    low = lambda r: r.astype(BF16)
    near = dot(low(o0[0]), wp0[...]) + dot(low(oc[0, 0]), low(wpc[0]))
    far = dot(low(ox[0]), low(wpx[...])) + dot(low(oc[1, 0]), low(wpc[1]))
    a = near + far + pb[...]
    a_ref[0] = a
    mid = tok_ref[0].astype(F32) + ls[0:1] * a
    mid_ref[0] = mid
    n2 = layer_norm(mid, gain[...], shift[...])[0].astype(BF16)
    u = dot(n2, w1[...]) + b1[...]
    cdf = 0.5 * (1.0 + lax.erf(u * np.float32(np.sqrt(0.5))))
    slope = cdf + u * (jnp.exp(-0.5 * u * u) * np.float32(1 / np.sqrt(2 * np.pi)))
    g = (u * cdf).astype(BF16)
    m = dot(g, w2[...])
    half = m.shape[1] // 2
    m_ref[0] = m[:, :half]
    m_ref[1] = m[:, half:]
    dm = (ls[1:2] * out_ref[0].astype(F32)).astype(BF16)
    du = (slope * dot_nt(dm, w2[...])).astype(BF16)
    dn = dot_nt(du, w1[...])
    dn_ref[0] = dn[:, :half]
    dn_ref[1] = dn[:, half:]
    d2 = dot_tn(g, dm)
    d1 = dot_tn(n2, du)
    s1 = column_sum(du.astype(F32))
    s2 = column_sum(dm.astype(F32))
    if not first:
        d2, d1, s1, s2 = d2 + a2[...], d1 + a1[...], s1 + ab1[...], s2 + ab2[...]
    d2_ref[...] = d2
    d1_ref[...] = d1
    db1_ref[...] = s1
    db2_ref[...] = s2


def once(spec_of, shape):
    spec = spec_of(shape)
    return pl.BlockSpec(spec.block_shape, spec.index_map, pipeline_mode=pl.Buffered(1))


def feed(scalars, tok3, out3, o_parts, w_parts, pb, ls, gain, shift, w1, b1, w2, sums):
    dim = tok3.shape[2]
    hid = w1.shape[1]
    width = w_parts[0].shape[0]
    first = sums is None
    pair = jax.ShapeDtypeStruct((2, LONG, dim // 2), F32)
    row = jax.ShapeDtypeStruct((1, LONG, dim), F32)
    sum_shapes = [(dim, hid), (hid, dim), (1, hid), (1, dim)]
    specs = [
        once(pack_spec, (LONG, dim)),
        once(pack_spec, (LONG, dim)),
        once(first_spec, (LONG, width)),
        once(first_spec, (LONG, width)),
        once(whole_spec, (2, 1, LONG, width)),
        once(whole_spec, (width, dim)),
        once(whole_spec, (width, dim)),
        once(whole_spec, (2, width, dim)),
        once(whole_spec, (1, dim)),
        once(whole_spec, (2, dim)),
        once(whole_spec, (1, dim)),
        once(whole_spec, (1, dim)),
        once(whole_spec, (dim, hid)),
        once(whole_spec, (1, hid)),
        once(whole_spec, (hid, dim)),
    ]
    if not first:
        specs += [once(whole_spec, s) for s in sum_shapes]
    return pl.pallas_call(
        partial(feed_kernel, first),
        out_shape=[row, row, pair, pair] + [jax.ShapeDtypeStruct(s, F32) for s in sum_shapes],
        grid_spec=pltpu.PrefetchScalarGridSpec(
            num_scalar_prefetch=1,
            grid=(1,),
            in_specs=specs,
            out_specs=[once(first_spec, (LONG, dim))] * 2
            + [once(whole_spec, pair.shape)] * 2
            + [once(whole_spec, s) for s in sum_shapes],
        ),
        compiler_params=params(),
        cost_estimate=pl.CostEstimate(
            flops=2 * LONG * dim * (dim + 6 * hid),
            transcendentals=2 * LONG * hid,
            bytes_accessed=30 * LONG * dim,
        ),
        name="feed",
    )(scalars, tok3, out3, *o_parts, *w_parts, pb, ls, gain, shift, w1, b1, w2, *(sums or ()))


def norm_back(upstream, unit_rows, inverse, gain_row):
    scaled = upstream * gain_row
    centred = scaled - jnp.mean(scaled, axis=-1, keepdims=True)
    centred = centred - unit_rows * jnp.mean(scaled * unit_rows, axis=-1, keepdims=True)
    return inverse * centred, column_sum(upstream * unit_rows), column_sum(upstream)


def joined(sc_ref, mine, peer):
    core = sc_ref[2]
    lo = jnp.where(core == 0, mine[...], peer[...])
    hi = jnp.where(core == 0, peer[...], mine[...])
    return jnp.concatenate([lo, hi], axis=1)


def middle_kernel(
    sc_ref, out_ref, mid_ref, a_ref, mine, peer, ls, gain, shift, wp0, wpx, o0, ox,
    dmid_ref, do0_ref, dox_ref, dp0_ref, dpx_ref, sum_ref
):
    dn2 = joined(sc_ref, mine, peer)
    _, unit, inverse = layer_norm(mid_ref[0], gain[...], shift[...])
    back, d_gain, d_shift = norm_back(dn2, unit, inverse, gain[...])
    dmid = out_ref[0].astype(F32) + back
    dmid_ref[0] = dmid
    da = (ls[0:1] * dmid).astype(BF16)
    do0_ref[0] = dot_nt(da, wp0[...]).astype(BF16).astype(F32)
    dox_ref[0] = dot_nt(da, wpx[...].astype(BF16)).astype(BF16).astype(F32)
    dp0_ref[...] = dot(o0[0].T.astype(BF16), da)
    dpx_ref[...] = dot(ox[0].T.astype(BF16), da)
    sum_ref[0:1] = d_gain
    sum_ref[1:2] = d_shift
    sum_ref[2:3] = column_sum(dmid * a_ref[0])
    sum_ref[3:4] = column_sum(da.astype(F32))


def middle_back(scalars, out3, mid, a, mine, peer, ls, gain, shift, w_parts, o_parts):
    dim = mid.shape[2]
    width = w_parts[0].shape[0]
    row = jax.ShapeDtypeStruct((1, LONG, dim), F32)
    low = jax.ShapeDtypeStruct((1, LONG, width), F32)
    mat = jax.ShapeDtypeStruct((width, dim), F32)
    return pl.pallas_call(
        middle_kernel,
        out_shape=[row, low, low, mat, mat, jax.ShapeDtypeStruct((4, dim), F32)],
        grid_spec=pltpu.PrefetchScalarGridSpec(
            num_scalar_prefetch=1,
            grid=(1,),
            in_specs=[
                once(pack_spec, (LONG, dim)),
                once(first_spec, (LONG, dim)),
                once(first_spec, (LONG, dim)),
                once(whole_spec, (LONG, dim // 2)),
                once(whole_spec, (LONG, dim // 2)),
                once(whole_spec, (2, dim)),
                once(whole_spec, (1, dim)),
                once(whole_spec, (1, dim)),
                once(whole_spec, (width, dim)),
                once(whole_spec, (width, dim)),
                once(first_spec, (LONG, width)),
                once(first_spec, (LONG, width)),
            ],
            out_specs=[
                once(first_spec, (LONG, dim)),
                once(first_spec, (LONG, width)),
                once(first_spec, (LONG, width)),
                once(whole_spec, (width, dim)),
                once(whole_spec, (width, dim)),
                once(whole_spec, (4, dim)),
            ],
        ),
        compiler_params=params(),
        cost_estimate=pl.CostEstimate(
            flops=8 * LONG * dim * width, transcendentals=LONG, bytes_accessed=24 * LONG * dim
        ),
        name="middle_back",
    )(scalars, out3, mid, a, mine, peer, ls, gain, shift, *w_parts[:2], *o_parts[:2])


def final_kernel(sc_ref, tok_ref, dmid_ref, mine, peer, gain, shift, out_ref, sum_ref):
    dn1 = joined(sc_ref, mine, peer)
    _, unit, inverse = layer_norm(tok_ref[0].astype(F32), gain[...], shift[...])
    back, d_gain, d_shift = norm_back(dn1, unit, inverse, gain[...])
    result = dmid_ref[0] + back
    half = result.shape[1] // 2
    out_ref[0] = result[:, :half]
    out_ref[1] = result[:, half:]
    sum_ref[0:1] = d_gain
    sum_ref[1:2] = d_shift


def final_back(scalars, tok3, dmid, mine, peer, gain, shift):
    dim = tok3.shape[2]
    return pl.pallas_call(
        final_kernel,
        out_shape=[
            jax.ShapeDtypeStruct((2, LONG, dim // 2), F32),
            jax.ShapeDtypeStruct((2, dim), F32),
        ],
        grid_spec=pltpu.PrefetchScalarGridSpec(
            num_scalar_prefetch=1,
            grid=(1,),
            in_specs=[
                once(pack_spec, (LONG, dim)),
                once(first_spec, (LONG, dim)),
                once(whole_spec, (LONG, dim // 2)),
                once(whole_spec, (LONG, dim // 2)),
                once(whole_spec, (1, dim)),
                once(whole_spec, (1, dim)),
            ],
            out_specs=[once(whole_spec, (2, LONG, dim // 2)), once(whole_spec, (2, dim))],
        ),
        compiler_params=params(),
        cost_estimate=pl.CostEstimate(
            flops=20 * LONG * dim, transcendentals=LONG, bytes_accessed=14 * LONG * dim
        ),
        name="final_back",
    )(scalars, tok3, dmid, mine, peer, gain, shift)


CORE = [(i, i ^ 1) for i in range(4)]
ACROSS = [(i, i ^ 2) for i in range(4)]


def to_core(x):
    return lax.ppermute(x, "narrow", CORE)


def to_chip(x):
    return lax.ppermute(x, "narrow", ACROSS)


def pick(pair, index):
    return lax.dynamic_index_in_dim(pair, index, 0, keepdims=False)


def chip_half(pair, core):
    return pick(pair, core) + to_core(pick(pair, 1 - core))


def small_sum(x, size):
    step = 1
    while step < size:
        x = x + lax.ppermute(x, "wide", [(i, i ^ step) for i in range(size)])
        step *= 2
    return x


def on_device(
    tokens, w_qkv, qv_bias, w_proj, proj_bias, w_fc1, fc1_bias, w_fc2, fc2_bias, norm_gains,
    norm_shifts, layer_scales, rel_table, image_ids, pad_mask, grid_rows, grid_cols, d_out, wide
):
    rows, dim = tokens.shape
    width = w_qkv.shape[2]
    heads = width // HD
    place = lax.axis_index("narrow")
    chip, core = place // 2, place % 2
    gains = norm_gains.astype(F32)
    shifts = norm_shifts.astype(F32)
    scales = layer_scales.astype(F32)
    tok3 = tokens.reshape(2, LONG, dim)
    out3 = d_out.reshape(2, LONG, dim)
    kinds = image_ids.reshape(2, LONG)[:, LONG - 1] % 2
    sc_far = jnp.stack([1 - chip, jnp.where(chip == 0, kinds[1], kinds[0]), core])
    sc_own = jnp.stack([chip, jnp.where(chip == 0, kinds[0], kinds[1]), core])

    wp_near = w_proj.astype(F32)
    wp_far = to_chip(wp_near)
    wp_pair = to_core(jnp.stack([wp_near, wp_far]))
    w_parts = (w_proj, wp_far, wp_pair)

    bias = make_bias(rel_table)
    qv = qv_bias.astype(F32)
    first = lambda sc: attend(sc, tok3, w_qkv, qv, gains[0:1], shifts[0:1], bias)
    o_far, *saved_far = first(sc_far)
    o_own, *saved_own = first(sc_own)
    x_own = to_chip(o_far)
    x_far = to_chip(o_own)
    far_parts = (o_far, x_far, to_core(jnp.stack([o_far, x_far])))
    own_parts = (o_own, x_own, to_core(jnp.stack([o_own, x_own])))

    pb = proj_bias.astype(F32)[None]
    b1 = fc1_bias.astype(F32)[None]
    common = (w_parts, pb, scales, gains[1:2], shifts[1:2], w_fc1, b1, w_fc2)
    mid_far, _, m_far, dn_far, *sums = feed(sc_far, tok3, out3, far_parts, *common, None)
    mid_own, a_own, m_own, dn_own, *sums = feed(sc_own, tok3, out3, own_parts, *common, sums)
    d_fc1, d_fc2, d_fc1_bias, d_fc2_bias = sums

    sent = to_chip(chip_half(dn_far, core))
    mine = chip_half(dn_own, core) + sent
    dmid, do_own, do_send, dp_own, dp_send, sums_two = middle_back(
        sc_own, out3, mid_own, a_own, mine, to_core(mine), scales, gains[1:2], shifts[1:2],
        w_parts, own_parts
    )
    do_far = to_chip(do_send)
    d_proj = dp_own + to_chip(dp_send)

    m_half_far = chip_half(m_far, core)
    m_half_own = chip_half(m_own, core)
    m_all_far = m_half_far + to_chip(m_half_own)
    m_all_own = m_half_own + to_chip(m_half_far)
    m_mine = jnp.where(chip == 0, jnp.stack([m_all_own, m_all_far]), jnp.stack([m_all_far, m_all_own]))
    m_peer = to_core(m_mine)
    m_full = jnp.where(
        core == 0,
        jnp.concatenate([m_mine, m_peer], axis=2),
        jnp.concatenate([m_peer, m_mine], axis=2),
    ) + fc2_bias.astype(F32)
    middle = jnp.where(
        chip == 0, jnp.concatenate([mid_own, mid_far]), jnp.concatenate([mid_far, mid_own])
    )
    block_out = (middle + scales[1] * m_full).astype(BF16).reshape(rows, dim)
    d_scale_two = jnp.sum(out3.astype(F32) * m_full, axis=(0, 1))

    (d_fc1, d_fc2) = lax.psum((d_fc1, d_fc2), "wide")

    back = lambda sc, saved, do, sums: attend_back(
        sc, tok3, w_qkv, gains[0:1], shifts[0:1], bias, saved, do, sums
    )
    dn_far, *sums = back(sc_far, saved_far, do_far, zero_sums(heads, dim, width))
    dn_own, *sums = back(sc_own, saved_own, do_own, sums)
    d_qkv, d_qv_bias, d_large, d_small, d_tails = sums
    sent = to_chip(chip_half(dn_far, core))
    mine = chip_half(dn_own, core) + sent
    tok_own, sums_one = final_back(
        sc_own, tok3, dmid, mine, to_core(mine), gains[0:1], shifts[0:1]
    )
    half_far = to_chip(pick(tok_own, core))
    both = jnp.stack([half_far, to_core(half_far)])
    far_lo = pick(both, core)
    far_hi = pick(both, 1 - core)
    tok_far = jnp.concatenate([far_lo, far_hi], axis=1)
    tok_own = jnp.concatenate([tok_own[0], tok_own[1]], axis=1)
    d_tokens = jnp.where(
        chip == 0, jnp.stack([tok_own, tok_far]), jnp.stack([tok_far, tok_own])
    ).reshape(rows, dim)

    d_table = strips_back(d_large, d_small, d_tails)
    own_rows = jnp.concatenate([sums_two, sums_one])
    own_rows = own_rows + to_chip(own_rows)
    hid = d_fc1_bias.shape[1]
    flat = jnp.concatenate(
        [
            own_rows.reshape(-1),
            d_fc2_bias.reshape(-1),
            d_scale_two,
            d_fc1_bias.reshape(-1),
            d_qv_bias.reshape(-1),
            d_table.reshape(-1),
        ]
    )
    count = flat.shape[0]
    lanes = 128
    flat = jnp.pad(flat, (0, -count % (8 * lanes))).reshape(-1, lanes)
    flat = small_sum(flat, wide).reshape(-1)
    own_rows = flat[: 6 * dim].reshape(6, dim)
    at = 6 * dim
    d_fc2_bias = flat[at : at + dim]
    d_scale_two = flat[at + dim : at + 2 * dim]
    at += 2 * dim
    d_fc1_bias = flat[at : at + hid]
    at += hid
    d_qv_bias = flat[at : at + 2 * width].reshape(2, width)
    at += 2 * width
    d_table = flat[at : at + d_table.size].reshape(d_table.shape)

    d_qkv, d_proj, d_fc1, d_fc2 = lax.optimization_barrier((d_qkv, d_proj, d_fc1, d_fc2))
    d_qkv, d_proj = lax.psum((d_qkv, d_proj), "wide")
    d_norm_gains = jnp.stack([own_rows[4], own_rows[0]])
    d_norm_shifts = jnp.stack([own_rows[5], own_rows[1]])
    d_layer_scales = jnp.stack([own_rows[2], d_scale_two])
    return (
        block_out,
        d_tokens,
        d_qkv,
        d_qv_bias,
        d_proj,
        own_rows[3],
        d_fc1,
        d_fc1_bias,
        d_fc2,
        d_fc2_bias,
        d_norm_gains,
        d_norm_shifts,
        d_layer_scales,
        d_table,
    )


def solution(mesh):
    in_specs = (
        P("wide", None),
        P(None, None, "narrow"),
        P(None, "narrow"),
        P("narrow", None),
        P(),
        P(None, "narrow"),
        P("narrow"),
        P("narrow", None),
        P(),
        P(),
        P(),
        P(),
        P("narrow", None),
        P("wide"),
        P("wide"),
        P("wide"),
        P("wide"),
        P("wide", None),
    )
    out_specs = (
        P("wide", None),
        P("wide", None),
        P(None, None, "narrow"),
        P(None, "narrow"),
        P("narrow", None),
        P(),
        P(None, "narrow"),
        P("narrow"),
        P("narrow", None),
        P(),
        P(),
        P(),
        P(),
        P("narrow", None),
    )
    return jax.shard_map(
        partial(on_device, wide=mesh.shape["wide"]),
        mesh=mesh,
        in_specs=in_specs,
        out_specs=out_specs,
        check_vma=False,
    )
```

time: 693 us -> 460 us (0.66)
  waiting for transfers between devices: 386 us -> 230 us
  matrix products: 131 us -> 5.63 us
  Pallas kernels: 0 us -> 92.1 us
  blocking collectives: 42 us -> 0 us
  starting transfers between devices: 0.34 us -> 16.3 us
  other arithmetic: 51.1 us -> 37.4 us
    psum x4 -> x2, waiting for transfers between devices: 386 us -> 117 us  [the longest x1 84.1 us: on_device(): d_qkv, d_proj = lax.psum((d_qkv, d_proj), 'wide')]
    dot_general x34 -> x4, matrix products: 129 us -> 5.63 us  [the longest x1 2.53 us: strips_back(): jnp.einsum('hsuc,ksc->huk', large, jnp.asarray(large_pick().reshape(2 * S...]
    ppermute x0 -> x27, waiting for transfers between devices: none -> 113 us  [the longest x11 101 us: to_chip(): return lax.ppermute(x, 'narrow', ACROSS)]
    pallas_call x0 -> x9, Pallas kernels: none -> 92.1 us  [the longest x2 29.4 us: attend_back(): pl.pallas_call(backward_kernel, out_shape=[jax.ShapeDtypeStruct((2, LONG,...]
    psum x1 -> x0, blocking collectives: 42 us -> none  [on_device(): lax.psum((d_qkv, d_qv_bias, d_proj, d_proj_bias, d_gain_one, d_shift_one,...]
    reduce_sum x15 -> x1, other arithmetic: 28.5 us -> 5.77 us  [on_device(): d_scale_two = jnp.sum(out3.astype(F32) * m_full, axis=(0, 1))]
    reshape x4 -> x14, local copies, waits for them, and re-layouts: 29.5 us -> 9.1 us  [the longest x1 1.6 us: strips_back(): small = d_small[:, :, 1:1 + rows * SMALL].reshape(heads, 16, rows, SMALL)]
    ppermute x0 -> x27, starting transfers between devices: none -> 16.2 us  [the longest x11 10.8 us: to_chip(): return lax.ppermute(x, 'narrow', ACROSS)]
  transfers between devices with their start and end apart: 4 -> 29, of which waited for: 4 -> 13; matrix products, arithmetic and copies ran while one was open for 15% -> 19% of each run, Pallas kernels for 0% -> 20%
where the time goes in v1:
time: 460 us; the launch traced here: 455 us
  waiting for transfers between devices  230 us (50%)
  Pallas kernels  92.1 us (20%)
  local copies, waits for them, and re-layouts  56.4 us (12%)
  other arithmetic  37.4 us (8%)
  between operations  17.5 us (4%)
  starting transfers between devices  16.3 us (4%)
  matrix products  5.63 us (1%)
    ppermute x11, waiting for transfers between devices, to_chip(): return lax.ppermute(x, 'narrow', ACROSS)  101 us
    psum x1, waiting for transfers between devices, on_device(): d_qkv, d_proj = lax.psum((d_qkv, d_proj), 'wide')  84.1 us
    psum x1, waiting for transfers between devices, on_device(): d_fc1, d_fc2 = lax.psum((d_fc1, d_fc2), 'wide')  33.2 us
    pallas_call x2, Pallas kernels, attend_back(): pl.pallas_call(backward_kernel, out_shape=[jax.ShapeDtypeStruct((2, LONG,...  29.4 us
    pallas_call x2, Pallas kernels, feed(): pl.pallas_call(partial(feed_kernel, first), out_shape=[row, row, pair, pa...  27.9 us
    pallas_call x2, Pallas kernels, attend(): pl.pallas_call(forward_kernel, out_shape=[jax.ShapeDtypeStruct((1, LONG,...  15 us
    unnamed x92, local copies, waits for them, and re-layouts  13.9 us
    ppermute x3, waiting for transfers between devices, small_sum(): x = x + lax.ppermute(x, 'wide', [(i, i ^ step) for i in range(size)])  11.1 us
  transfers between devices with their start and end apart: 29, of which 13 were waited for; matrix products, arithmetic and copies ran while one was open for 19% of the time, Pallas kernels for 20%

profile of v1, /device:TPU:0, one launch (start us, length us, event | category | flops | bytes accessed | tf_op | source)
XLA Modules:
  0.0 455.3 jit_solution(10536703457729479990)
XLA Ops:
  7.2 2.0 convert_bitcast_fusion
  9.3 2.9 collective-permute-start.2
  13.2 1.3 slice_convert_fusion.tail_ref
  15.4 1.3 fusion.12
  17.2 1.6 reshape.133
  21.6 1.6 copy.68.w_ref
  25.7 6.1 %bias.1.bias_ref = bf16[2,3,584,584]{3,2,1,0:T(8,128)(2,1)} custom-call(f32[3,3]{1,0:T(4,128)} %slice_convert_fusion.tail_ref, f32[3,24,1280]{2,1,0:T(8,128)} %pad.26.large_ref, f32[3,16,640]{2,1,0:T(8,128)} %pad.27.small_ref), custom_call_target="tpu_custom_call" | custom-call | tf_op jit(solution)/shard_map/bias/pallas_call | solution.py:142
  33.0 7.6 %attend.2 = (f32[1,584,192]{2,1,0:T(8,128)}, bf16[1,584,192]{2,1,0:T(8,128)(2,1)}, bf16[1,584,192]{2,1,0:T(8,128)(2,1)}, bf16[1,584,192]{2,1,0:T(8,128)(2,1)}, f32[1,3,584]{2,1,0:T(4,128)}) custom-call(s32[3]{0:T(128)} %add_add_fusion.sc_ref.refs_0_, bf16[2,584,768]{2,1,0:T(8,128)(2,1)} %bitcast.151, bf16[3,768,192]{2,1,0:T(8,128)(2,1)} %copy.68.w_ref, ...), custom_call_target="tpu_custom_call" | custom-call | flops 778616832 | bytes 5634432 | tf_op jit(solution)/shard_map/attend/pallas_call | solution.py:220
  40.6 1.3 copy.73
  43.3 1.2 pad_maximum_fusion.2
  45.0 7.5 %attend.3 = (f32[1,584,192]{2,1,0:T(8,128)}, bf16[1,584,192]{2,1,0:T(8,128)(2,1)}, bf16[1,584,192]{2,1,0:T(8,128)(2,1)}, bf16[1,584,192]{2,1,0:T(8,128)(2,1)}, f32[1,3,584]{2,1,0:T(4,128)}) custom-call(s32[3]{0:T(128)} %add_add_fusion.1.sc_ref.refs_0_, bf16[2,584,768]{2,1,0:T(8,128)(2,1)} %bitcast.152, bf16[3,768,192]{2,1,0:T(8,128)(2,1)} %copy.68.w_ref, ...), custom_call_target="tpu_custom_call" | custom-call | flops 778616832 | bytes 5634432 | tf_op jit(solution)/shard_map/attend/pallas_call | solution.py:220
  52.5 2.1 collective-permute-done.4
  55.7 1.2 pad_maximum_fusion.1
  56.9 1.3 copy.75
  58.9 13.2 %collective-permute-done = f32[1,584,192]{1,2,0:T(8,128)S(1)} collective-permute-done((f32[1,584,192]{1,2,0:T(8,128)S(1)}, f32[1,584,192]{1,2,0:T(8,128)S(1)}, u32[]{:S(2)}, u32[]{:S(2)}) %collective-permute-start) | collective-permute-done | bytes 448544 | tf_op jit(solution)/shard_map/ppermute | solution.py:651
  75.0 2.6 copy.77.refs_5_
  77.6 13.1 %feed.2 = (f32[1,584,768]{2,1,0:T(8,128)}, f32[1,584,768]{2,1,0:T(8,128)}, f32[2,584,384]{2,1,0:T(8,128)}, f32[2,584,384]{2,1,0:T(8,128)}, f32[768,768]{1,0:T(8,...) custom-call(s32[3]{0:T(128)} %add_add_fusion.1.sc_ref.refs_0_, bf16[2,584,768]{2,1,0:T(8,128)(2,1)} %bitcast.153, ...), custom_call_target="tpu_custom_call" | custom-call | flops 4822401024 | bytes 13455360 | tf_op jit(solution)/shard_map/feed/pallas_call | solution.py:503
  90.7 2.2 dynamic-slice_bitcast_fusion.3
  93.3 1.4 copy.79.refs_5_
  94.8 14.8 %feed.3 = (f32[1,584,768]{2,1,0:T(8,128)}, f32[1,584,768]{2,1,0:T(8,128)}, f32[2,584,384]{2,1,0:T(8,128)}, f32[2,584,384]{2,1,0:T(8,128)}, f32[768,768]{1,0:T(8,...) custom-call(s32[3]{0:T(128)} %add_add_fusion.sc_ref.refs_0_, bf16[2,584,768]{2,1,0:T(8,128)(2,1)} %bitcast.154, ...), custom_call_target="tpu_custom_call" | custom-call | flops 4822401024 | bytes 13455360 | tf_op jit(solution)/shard_map/feed/pallas_call | solution.py:503
  109.6 1.4 dynamic-slice_bitcast_fusion.4
  114.4 1.3 collective-permute-start.8
  115.7 19.6 %collective-permute-done.13 = f32[584,384]{1,0:T(8,128)S(1)} collective-permute-done((f32[584,384]{1,0:T(8,128)S(1)}, f32[584,384]{1,0:T(8,128)S(1)}, u32[]{:S(2)}, u32[]{:S(2)}) %collective-permute-start.13) | collective-permute-done | bytes 897056 | tf_op jit(solution)/shard_map/ppermute | solution.py:651
  137.3 16.4 %collective-permute-done.8 = f32[584,384]{1,0:T(8,128)} collective-permute-done((f32[584,384]{1,0:T(8,128)S(1)}, f32[584,384]{1,0:T(8,128)}, u32[]{:S(2)}, u32[]{:S(2)}) %collective-permute-start.8) | collective-permute-done | bytes 897056 | tf_op jit(solution)/shard_map/ppermute | solution.py:651
  153.8 2.8 add_bitcast_fusion.1
  156.8 8.0 %middle_back.1 = (f32[1,584,768]{2,1,0:T(8,128)}, f32[1,584,192]{2,1,0:T(8,128)}, f32[1,584,192]{2,1,0:T(8,128)}, f32[192,768]{1,0:T(8,128)}, f32[192,768]{1,0:T(8,128)}, /*index=5*/f32[4,768]{1,0:T(4,128)}) custom-call(s32[3]{0:T(128)} %add_add_fusion.sc_ref.refs_0_, bf16[2,584,768]{2,1,0:T(8,128)(2,1)} %bitcast.160, ...), custom_call_target="tpu_custom_call" | custom-call | flops 688914432 | bytes 10764288 | tf_op jit(solution)/shard_map/middle_back/pallas_call | solution.py:564
  164.8 1.3 copy.81
  166.1 1.8 collective-permute-start.15
  167.9 20.4 %collective-permute-done.15 = f32[1,584,192]{1,2,0:T(8,128)S(1)} collective-permute-done((f32[1,584,192]{1,2,0:T(8,128)S(1)}, f32[1,584,192]{1,2,0:T(8,128)S(1)}, u32[]{:S(2)}, u32[]{:S(2)}) %collective-permute-start.15) | collective-permute-done | bytes 448544 | tf_op jit(solution)/shard_map/ppermute | solution.py:651
  189.4 1.6 broadcast_in_dim.30.aw_ref
  193.6 14.8 %attend_back.2 = (f32[2,584,384]{2,1,0:T(8,128)}, f32[3,768,192]{2,1,0:T(8,128)}, f32[2,192]{1,0:T(2,128)}, f32[3,24,1280]{2,1,0:T(8,128)}, f32[3,16,640]{2,1,0:T(8,128)}, /*index=5*/f32[3,8,128]{2,1,0:T(8,128)}) custom-call(s32[3]{0:T(128)} %add_add_fusion.1.sc_ref.refs_0_, bf16[2,584,768]{2,1,0:T(8,128)(2,1)} %bitcast.155, ...), custom_call_target="tpu_custom_call" | custom-call | flops 1688199168 | bytes 9222528 | tf_op jit(solution)/shard_map/attend_back/pallas_call | solution.py:380
  208.4 1.2 dynamic-slice_bitcast_fusion.1
  209.7 1.3 add_bitcast_fusion
  211.0 1.4 maximum_select_fusion.3
  212.8 14.6 %attend_back.3 = (f32[2,584,384]{2,1,0:T(8,128)}, f32[3,768,192]{2,1,0:T(8,128)}, f32[2,192]{1,0:T(2,128)}, f32[3,24,1280]{2,1,0:T(8,128)}, f32[3,16,640]{2,1,0:T(8,128)}, /*index=5*/f32[3,8,128]{2,1,0:T(8,128)}) custom-call(s32[3]{0:T(128)} %add_add_fusion.sc_ref.refs_0_, bf16[2,584,768]{2,1,0:T(8,128)(2,1)} %bitcast.156, bf16[3,768,192]{2,1,0:T(8,128)(2,1)} %copy.68.w_ref, ...), custom_call_target="tpu_custom_call" | custom-call | flops 1688199168 | bytes 9222528 | tf_op jit(solution)/shard_map/attend_back/pallas_call | solution.py:380
  227.4 2.4 dynamic-slice_bitcast_fusion.2
  231.7 4.2 maximum_select_fusion
  236.0 1.6 collective-permute-start.22
  238.9 1.6 slice.147
  240.5 1.6 reshape.141
  242.1 1.7 convolution_bitcast_fusion.2
  243.8 2.5 convolution_bitcast_fusion.1
  247.3 5.6 %collective-permute-done.18 = f32[584,384]{1,0:T(8,128)} collective-permute-done((f32[584,384]{1,0:T(8,128)S(1)}, f32[584,384]{1,0:T(8,128)}, u32[]{:S(2)}, u32[]{:S(2)}) %collective-permute-start.18) | collective-permute-done | bytes 897056 | tf_op jit(solution)/shard_map/ppermute | solution.py:651
  252.9 2.0 fusion.6.mine
  255.2 1.2 reshape.139
  256.4 8.7 %collective-permute-done.22 = f32[192,768]{1,0:T(8,128)} collective-permute-done((f32[192,768]{1,0:T(8,128)}, f32[192,768]{1,0:T(8,128)}, u32[]{:S(2)}, u32[]{:S(2)}) %collective-permute-start.22) | collective-permute-done | bytes 589856 | tf_op jit(solution)/shard_map/ppermute | solution.py:651
  265.1 2.1 add.134
  267.2 5.8 %multiply_reduce_fusion = (f32[768]{0:T(1024)S(1)}, bf16[1168,768]{1,0:T(8,128)(2,1)}) fusion(bf16[1168,768]{1,0:T(8,128)(2,1)S(1)} %copy-done.1, f32[1168,384]{1,0:T(8,128)} %bitcast.28, f32[1168,384]{1,0:T(8,128)} %bitcast.29, f32[768]{0:T(1024)S(1)} %convert_element_type.49, pred[]{:T(512)S(6)} %eq.9, f32[768]{0:T(1024)S(1)} %slice_reduce_fusion, ...), kind=kLoop, calls=%fused_computation.6 | loop fusion | flops 8969472 | bytes 10773505 | tf_op jit(solution)/shard_map/reduce_sum | solution.py:734
  273.0 33.2 %all-reduce.13.cloned.1.call-done = (f32[768,768]{1,0:T(8,128)}, f32[768,768]{1,0:T(8,128)}) async-done(((f32[768,768]{1,0:T(8,128)}, f32[768,768]{1,0:T(8,128)}), (f32[768,768]{1,0:T(8,128)}, f32[768,768]{1,0:T(8,128)})) %all-reduce.13.cloned.1.call-update) | async-done | bytes 4718608 | tf_op jit(solution)/shard_map/psum | solution.py:736
  306.2 5.6 %final_back.1 = (f32[2,584,384]{2,1,0:T(8,128)}, f32[2,768]{1,0:T(2,128)}) custom-call(s32[3]{0:T(128)} %add_add_fusion.sc_ref.refs_0_, bf16[2,584,768]{2,1,0:T(8,128)(2,1)} %bitcast.157, f32[1,584,768]{2,1,0:T(8,128)} %get-tuple-element.76.dmid_ref, f32[584,384]{1,0:T(8,128)} %copy-done.5, f32[584,384]{1,0:T(8,128)} %collective-permute-done.19.peer, ...), custom_call_target="tpu_custom_call" | custom-call | flops 8970240 | bytes 6279168 | tf_op jit(solution)/shard_map/final_back/pallas_call | solution.py:615
  312.6 1.5 collective-permute-start.23
  314.1 3.3 slice_bitcast_fusion.1
  317.7 1.5 collective-permute-start.24
  319.2 3.9 collective-permute-done.24
  323.2 15.2 %collective-permute-done.20 = f32[584,384]{1,0:T(8,128)} collective-permute-done((f32[584,384]{1,0:T(8,128)S(1)}, f32[584,384]{1,0:T(8,128)}, u32[]{:S(2)}, u32[]{:S(2)}) %collective-permute-start.20) | collective-permute-done | bytes 897056 | tf_op jit(solution)/shard_map/ppermute | solution.py:651
  338.4 1.5 collective-permute-start.26
  339.9 1.3 maximum_bitcast_fusion
  341.3 7.1 %collective-permute-done.26 = f32[112,128]{1,0:T(8,128)S(1)} collective-permute-done((f32[112,128]{1,0:T(8,128)S(1)}, f32[112,128]{1,0:T(8,128)S(1)}, u32[]{:S(2)}, u32[]{:S(2)}) %collective-permute-start.26) | collective-permute-done | bytes 57376 | tf_op jit(solution)/shard_map/ppermute | solution.py:665
  352.3 84.1 %all-reduce.11.cloned.1.call-done = (f32[3,768,192]{2,1,0:T(8,128)}, f32[192,768]{1,0:T(8,128)}) async-done(((f32[3,768,192]{2,1,0:T(8,128)}, f32[192,768]{1,0:T(8,128)}), (f32[3,768,192]{2,1,0:T(8,128)}, f32[192,768]{1,0:T(8,128)})) %all-reduce.11.cloned.1.call-update) | async-done | bytes 2359312 | tf_op jit(solution)/shard_map/psum | solution.py:789
  436.3 2.9 copy.87
  439.2 1.6 fusion.5
  441.0 2.1 maximum_select_fusion.2
  444.4 1.4 copy.125
  446.9 1.4 copy.126
  (193 shorter events, 34.7 us)
Async XLA Ops:
  7.2 299.0 %all-reduce.13.cloned.1.call-start = ((), (), s32[]{:S(2)}) async-start(), calls=%async_computation.1 | async-start | bytes 9437184 | tf_op jit(solution)/shard_map/psum | solution.py:736
  9.3 34.0 %collective-permute-start.2 = (f32[192,768]{1,0:T(8,128)}, f32[192,768]{1,0:T(8,128)S(1)}, u32[]{:S(2)}, u32[]{:S(2)}) collective-permute-start(f32[192,768]{1,0:T(8,128)} %get-tuple-element.182), channel_id=1, source_target_pairs={{0,2},{1,3},{2,0},{3,1},{4,6},{5,7},{6,4},{7,5},{8,10},{9,11},{10,... | collective-permute-start | bytes 1769480 | tf_op jit(solution)/shard_map/ppermute | solution.py:651
  16.6 2.1 copy-start.24
  18.8 1.2 copy-start.17
  19.1 2.5 copy-start.19
  19.6 3.6 copy-start.36
  25.7 6.8 %copy-start.28 = (bf16[2,768]{1,0:T(2,128)(2,1)S(1)}, bf16[2,768]{1,0:T(2,128)(2,1)}, u32[]{:S(2)}) copy-start(bf16[2,768]{1,0:T(2,128)(2,1)} %param.32) | copy-start | bytes 9220
  25.7 6.8 %copy-start.29 = (bf16[2,768]{1,0:T(2,128)(2,1)S(1)}, bf16[2,768]{1,0:T(2,128)(2,1)}, u32[]{:S(2)}) copy-start(bf16[2,768]{1,0:T(2,128)(2,1)} %param.31) | copy-start | bytes 9220
  33.0 10.3 %copy-start.11 = (f32[1,192,768]{2,1,0:T(8,128)S(1)}, f32[1,192,768]{2,1,0:T(8,128)}, u32[]{:S(2)}) copy-start(f32[1,192,768]{2,1,0:T(8,128)} %get-tuple-element.181) | copy-start | bytes 1769476
  41.9 12.7 %collective-permute-start.4 = (f32[1,584,192]{1,2,0:T(8,128)S(1)}, f32[1,584,192]{1,2,0:T(8,128)S(1)}, u32[]{:S(2)}, u32[]{:S(2)}) collective-permute-start(f32[1,584,192]{1,2,0:T(8,128)S(1)} %copy.73), channel_id=1, source_target_pairs={{0,2},{1,3},{2,0},{3,1},{4,6},{5,7},{6,4},{7,5},{8,10},{9,11},{10,... | collective-permute-start | bytes 1345544 | tf_op jit(solution)/shard_map/ppermute | solution.py:651
  43.3 9.2 %copy-start.8 = (f32[192,768]{1,0:T(8,128)}, f32[192,768]{1,0:T(8,128)S(1)}, u32[]{:S(2)}) copy-start(f32[192,768]{1,0:T(8,128)S(1)} %collective-permute-done.2.refs_7_.wpx) | copy-start | bytes 1769476
  44.5 33.1 %collective-permute-start.3 = (f32[2,192,768]{2,1,0:T(8,128)}, f32[2,192,768]{2,1,0:T(8,128)}, u32[]{:S(2)}, u32[]{:S(2)}) collective-permute-start(f32[2,192,768]{2,1,0:T(8,128)} %pad_maximum_fusion.2), channel_id=1, source_target_pairs={{0,1},{1,0},{2,3},{3,2},{4,5},{5,4},{6,7},{7,6},{8,9},{9,8},{10,11... | collective-permute-start | bytes 3538952 | tf_op jit(solution)/shard_map/ppermute | solution.py:647
  54.9 0.8 copy-start.7
  55.7 2.6 copy-start.6
  56.9 15.5 %copy-start.2 = (f32[1,584,192]{2,1,0:T(8,128)S(1)}, f32[1,584,192]{2,1,0:T(8,128)}, u32[]{:S(2)}) copy-start(f32[1,584,192]{2,1,0:T(8,128)} %get-tuple-element.63.refs_3_.o0) | copy-start | bytes 1345540
  58.2 16.7 %collective-permute-start.5 = (f32[2,1,584,192]{2,3,1,0:T(8,128)}, f32[2,1,584,192]{2,3,1,0:T(8,128)}, u32[]{:S(2)}, u32[]{:S(2)}) collective-permute-start(f32[2,1,584,192]{2,3,1,0:T(8,128)} %copy.75), channel_id=1, source_target_pairs={{0,1},{1,0},{2,3},{3,2},{4,5},{5,4},{6,7},{7,6},{8,9},{9,8},{10,11... | collective-permute-start | bytes 2691080 | tf_op jit(solution)/shard_map/ppermute | solution.py:647
  58.5 13.7 %collective-permute-start = (f32[1,584,192]{1,2,0:T(8,128)S(1)}, f32[1,584,192]{1,2,0:T(8,128)S(1)}, u32[]{:S(2)}, u32[]{:S(2)}) collective-permute-start(f32[1,584,192]{1,2,0:T(8,128)S(1)} %copy.70), channel_id=1, source_target_pairs={{0,2},{1,3},{2,0},{3,1},{4,6},{5,7},{6,4},{7,5},{8,10},{9,11},{10,... | collective-permute-start | bytes 1345544 | tf_op jit(solution)/shard_map/ppermute | solution.py:651
  72.4 0.8 copy-start.3
  72.4 0.8 copy-start.30
  72.4 1.4 copy-start.34
  72.4 2.0 copy-start.35
  73.2 20.1 %collective-permute-start.1 = (f32[2,1,584,192]{2,3,1,0:T(8,128)S(1)}, f32[2,1,584,192]{2,3,1,0:T(8,128)S(1)}, u32[]{:S(2)}, u32[]{:S(2)}) collective-permute-start(f32[2,1,584,192]{2,3,1,0:T(8,128)S(1)} %copy.72), channel_id=1, source_target_pairs={{0,1},{1,0},{2,3},{3,2},{4,5},{5,4},{6,7},{7,6},{8,9},{9,8},{10,11... | collective-permute-start | bytes 2691080 | tf_op jit(solution)/shard_map/ppermute | solution.py:647
  92.8 19.5 %collective-permute-start.12 = (f32[584,384]{1,0:T(8,128)}, f32[584,384]{1,0:T(8,128)S(1)}, u32[]{:S(2)}, u32[]{:S(2)}) collective-permute-start(f32[584,384]{1,0:T(8,128)} %dynamic-slice_bitcast_fusion.3), channel_id=1, source_target_pairs={{0,1},{1,0},{2,3},{3,2},{4,5},{5,4},{6,7},{7,6},{8,9},{9,8},{10,11... | collective-permute-start | bytes 2691080 | tf_op jit(solution)/shard_map/ppermute | solution.py:647
  109.6 1.8 copy-start.13
  109.6 2.8 copy-start.15
  111.4 1.6 copy-start.12
  111.4 2.9 collective-permute-start.7
  111.9 3.9 collective-permute-start.11
  112.5 22.8 %collective-permute-start.13 = (f32[584,384]{1,0:T(8,128)S(1)}, f32[584,384]{1,0:T(8,128)S(1)}, u32[]{:S(2)}, u32[]{:S(2)}) collective-permute-start(f32[584,384]{1,0:T(8,128)S(1)} %bitcast_add_fusion.3), channel_id=1, source_target_pairs={{0,2},{1,3},{2,0},{3,1},{4,6},{5,7},{6,4},{7,5},{8,10},{9,11},{10,... | collective-permute-start | bytes 2691080 | tf_op jit(solution)/shard_map/ppermute | solution.py:651
  113.9 21.4 %copy-start.16 = (f32[2,584,384]{2,1,0:T(8,128)S(1)}, f32[2,584,384]{2,1,0:T(8,128)}, u32[]{:S(2)}) copy-start(f32[2,584,384]{2,1,0:T(8,128)} %get-tuple-element.74) | copy-start | bytes 5382148
  114.0 22.4 %collective-permute-start.6 = (f32[584,384]{1,0:T(8,128)}, f32[584,384]{1,0:T(8,128)S(1)}, u32[]{:S(2)}, u32[]{:S(2)}) collective-permute-start(f32[584,384]{1,0:T(8,128)} %dynamic-slice_bitcast_fusion.6), channel_id=1, source_target_pairs={{0,1},{1,0},{2,3},{3,2},{4,5},{5,4},{6,7},{7,6},{8,9},{9,8},{10,11... | collective-permute-start | bytes 2691080 | tf_op jit(solution)/shard_map/ppermute | solution.py:647
  114.4 39.4 %collective-permute-start.8 = (f32[584,384]{1,0:T(8,128)S(1)}, f32[584,384]{1,0:T(8,128)}, u32[]{:S(2)}, u32[]{:S(2)}) collective-permute-start(f32[584,384]{1,0:T(8,128)S(1)} %bitcast_add_fusion.5), channel_id=1, source_target_pairs={{0,2},{1,3},{2,0},{3,1},{4,6},{5,7},{6,4},{7,5},{8,10},{9,11},{10,... | collective-permute-start | bytes 2691080 | tf_op jit(solution)/shard_map/ppermute | solution.py:651
  135.5 0.9 copy-start.4
  135.5 21.4 %collective-permute-start.14 = (f32[584,384]{1,0:T(8,128)S(1)}, f32[584,384]{1,0:T(8,128)}, u32[]{:S(2)}, u32[]{:S(2)}) collective-permute-start(f32[584,384]{1,0:T(8,128)S(1)} %fusion.7.mine), channel_id=1, source_target_pairs={{0,1},{1,0},{2,3},{3,2},{4,5},{5,4},{6,7},{7,6},{8,9},{9,8},{10,11... | collective-permute-start | bytes 2691080 | tf_op jit(solution)/shard_map/ppermute | solution.py:647
  136.4 299.9 %all-reduce.11.cloned.1.call-start = ((), (), s32[]{:S(2)}) async-start(), calls=%async_computation | async-start | bytes 5898240 | tf_op jit(solution)/shard_map/psum | solution.py:789
  136.4 0.9 copy-start.18
  156.6 53.1 %collective-permute-start.9 = (f32[584,384]{1,0:T(8,128)}, f32[584,384]{1,0:T(8,128)}, u32[]{:S(2)}, u32[]{:S(2)}) collective-permute-start(f32[584,384]{1,0:T(8,128)} %get-tuple-element.173), channel_id=1, source_target_pairs={{0,2},{1,3},{2,0},{3,1},{4,6},{5,7},{6,4},{7,5},{8,10},{9,11},{10,... | collective-permute-start | bytes 2691080 | tf_op jit(solution)/shard_map/ppermute | solution.py:651
  166.1 22.2 %collective-permute-start.15 = (f32[1,584,192]{1,2,0:T(8,128)S(1)}, f32[1,584,192]{1,2,0:T(8,128)S(1)}, u32[]{:S(2)}, u32[]{:S(2)}) collective-permute-start(f32[1,584,192]{1,2,0:T(8,128)S(1)} %copy.81), channel_id=1, source_target_pairs={{0,2},{1,3},{2,0},{3,1},{4,6},{5,7},{6,4},{7,5},{8,10},{9,11},{10,... | collective-permute-start | bytes 1345544 | tf_op jit(solution)/shard_map/ppermute | solution.py:651
  209.6 20.3 %collective-permute-start.17 = (f32[584,384]{1,0:T(8,128)S(1)}, f32[584,384]{1,0:T(8,128)S(1)}, u32[]{:S(2)}, u32[]{:S(2)}) collective-permute-start(f32[584,384]{1,0:T(8,128)S(1)} %dynamic-slice_bitcast_fusion.1), channel_id=1, source_target_pairs={{0,1},{1,0},{2,3},{3,2},{4,5},{5,4},{6,7},{7,6},{8,9},{9,8},{10,11... | collective-permute-start | bytes 2691080 | tf_op jit(solution)/shard_map/ppermute | solution.py:647
  212.3 54.9 %collective-permute-start.10 = (f32[2,584,384]{2,1,0:T(8,128)}, f32[2,584,384]{2,1,0:T(8,128)}, u32[]{:S(2)}, u32[]{:S(2)}) collective-permute-start(f32[2,584,384]{2,1,0:T(8,128)} %maximum_select_fusion.3), channel_id=1, source_target_pairs={{0,1},{1,0},{2,3},{3,2},{4,5},{5,4},{6,7},{7,6},{8,9},{9,8},{10,11... | collective-permute-start | bytes 5382152 | tf_op jit(solution)/shard_map/ppermute | solution.py:647
  227.4 2.5 copy-start.14
  229.8 0.7 copy-start.32
  229.8 1.3 copy-start.31
  229.8 1.9 copy-start
  229.8 17.5 %collective-permute-start.16 = (f32[584,384]{1,0:T(8,128)}, f32[584,384]{1,0:T(8,128)}, u32[]{:S(2)}, u32[]{:S(2)}) collective-permute-start(f32[584,384]{1,0:T(8,128)} %dynamic-slice_bitcast_fusion.2), channel_id=1, source_target_pairs={{0,1},{1,0},{2,3},{3,2},{4,5},{5,4},{6,7},{7,6},{8,9},{9,8},{10,11... | collective-permute-start | bytes 2691080 | tf_op jit(solution)/shard_map/ppermute | solution.py:647
  230.0 22.9 %collective-permute-start.18 = (f32[584,384]{1,0:T(8,128)S(1)}, f32[584,384]{1,0:T(8,128)}, u32[]{:S(2)}, u32[]{:S(2)}) collective-permute-start(f32[584,384]{1,0:T(8,128)S(1)} %bitcast_add_fusion.1), channel_id=1, source_target_pairs={{0,2},{1,3},{2,0},{3,1},{4,6},{5,7},{6,4},{7,5},{8,10},{9,11},{10,... | collective-permute-start | bytes 2691080 | tf_op jit(solution)/shard_map/ppermute | solution.py:651
  231.7 5.9 %copy-start.21 = (f32[3,24,1280]{2,1,0:T(8,128)S(1)}, f32[3,24,1280]{2,1,0:T(8,128)}, u32[]{:S(2)}) copy-start(f32[3,24,1280]{2,1,0:T(8,128)} %get-tuple-element.106) | copy-start | bytes 1105924
  236.0 29.1 %collective-permute-start.22 = (f32[192,768]{1,0:T(8,128)}, f32[192,768]{1,0:T(8,128)}, u32[]{:S(2)}, u32[]{:S(2)}) collective-permute-start(f32[192,768]{1,0:T(8,128)} %get-tuple-element.97), channel_id=1, source_target_pairs={{0,2},{1,3},{2,0},{3,1},{4,6},{5,7},{6,4},{7,5},{8,10},{9,11},{10,... | collective-permute-start | bytes 1769480 | tf_op jit(solution)/shard_map/ppermute | solution.py:651
  254.9 18.1 %copy-start.5 = (f32[584,384]{1,0:T(8,128)}, f32[584,384]{1,0:T(8,128)S(1)}, u32[]{:S(2)}) copy-start(f32[584,384]{1,0:T(8,128)S(1)} %fusion.6.mine) | copy-start | bytes 2691076
  254.9 12.3 %copy-start.1 = (bf16[1168,768]{1,0:T(8,128)(2,1)S(1)}, bf16[1168,768]{1,0:T(8,128)(2,1)}, u32[]{:S(2)}) copy-start(bf16[1168,768]{1,0:T(8,128)(2,1)} %param.36) | copy-start | bytes 5382148
  254.9 51.3 %collective-permute-start.19 = (f32[584,384]{1,0:T(8,128)S(1)}, f32[584,384]{1,0:T(8,128)}, u32[]{:S(2)}, u32[]{:S(2)}) collective-permute-start(f32[584,384]{1,0:T(8,128)S(1)} %fusion.6.mine), channel_id=1, source_target_pairs={{0,1},{1,0},{2,3},{3,2},{4,5},{5,4},{6,7},{7,6},{8,9},{9,8},{10,11... | collective-permute-start | bytes 2691080 | tf_op jit(solution)/shard_map/ppermute | solution.py:647
  306.2 5.7 %copy-start.22 = (f32[4,768]{1,0:T(4,128)S(1)}, f32[4,768]{1,0:T(4,128)}, u32[]{:S(2)}) copy-start(f32[4,768]{1,0:T(4,128)} %get-tuple-element.101) | copy-start | bytes 36868
  312.6 4.9 %collective-permute-start.23 = (f32[6,768]{1,0:T(8,128)S(1)}, f32[6,768]{1,0:T(8,128)S(1)}, u32[]{:S(2)}, u32[]{:S(2)}) collective-permute-start(f32[6,768]{1,0:T(8,128)S(1)} %pad_maximum_fusion.4), channel_id=1, source_target_pairs={{0,2},{1,3},{2,0},{3,1},{4,6},{5,7},{6,4},{7,5},{8,10},{9,11},{10,... | collective-permute-start | bytes 55304 | tf_op jit(solution)/shard_map/ppermute | solution.py:651
  314.1 3.4 copy-start.25
  314.1 3.5 copy-start.27
  314.1 3.5 copy-start.26
  317.5 20.9 %collective-permute-start.20 = (f32[584,384]{1,0:T(8,128)S(1)}, f32[584,384]{1,0:T(8,128)}, u32[]{:S(2)}, u32[]{:S(2)}) collective-permute-start(f32[584,384]{1,0:T(8,128)S(1)} %get-tuple-element.177), channel_id=1, source_target_pairs={{0,2},{1,3},{2,0},{3,1},{4,6},{5,7},{6,4},{7,5},{8,10},{9,11},{10,... | collective-permute-start | bytes 2691080 | tf_op jit(solution)/shard_map/ppermute | solution.py:651
  317.7 5.5 %collective-permute-start.24 = (f32[112,128]{1,0:T(8,128)S(1)}, f32[112,128]{1,0:T(8,128)S(1)}, u32[]{:S(2)}, u32[]{:S(2)}) collective-permute-start(f32[112,128]{1,0:T(8,128)S(1)} %pad_bitcast_fusion), channel_id=1, source_target_pairs={{0,4},{4,0},{8,12},{12,8},{16,20},{20,16},{24,28},{28,24},{1,5},{5... | collective-permute-start | bytes 172040 | tf_op jit(solution)/shard_map/ppermute | solution.py:665
  323.2 15.3 %collective-permute-start.25 = (f32[112,128]{1,0:T(8,128)S(1)}, f32[112,128]{1,0:T(8,128)S(1)}, u32[]{:S(2)}, u32[]{:S(2)}) collective-permute-start(f32[112,128]{1,0:T(8,128)S(1)} %fusion.25), channel_id=1, source_target_pairs={{0,8},{4,12},{8,0},{12,4},{16,24},{20,28},{24,16},{28,20},{1,9},{5... | collective-permute-start | bytes 172040 | tf_op jit(solution)/shard_map/ppermute | solution.py:665
  338.4 100.8 %collective-permute-start.21 = (f32[584,384]{1,0:T(8,128)}, f32[584,384]{1,0:T(8,128)}, u32[]{:S(2)}, u32[]{:S(2)}) collective-permute-start(f32[584,384]{1,0:T(8,128)} %collective-permute-done.20), channel_id=1, source_target_pairs={{0,1},{1,0},{2,3},{3,2},{4,5},{5,4},{6,7},{7,6},{8,9},{9,8},{10,11... | collective-permute-start | bytes 2691080 | tf_op jit(solution)/shard_map/ppermute | solution.py:647
  338.4 10.0 %collective-permute-start.26 = (f32[112,128]{1,0:T(8,128)S(1)}, f32[112,128]{1,0:T(8,128)S(1)}, u32[]{:S(2)}, u32[]{:S(2)}) collective-permute-start(f32[112,128]{1,0:T(8,128)S(1)} %fusion.35), channel_id=1, source_target_pairs={{0,16},{4,20},{8,24},{12,28},{16,0},{20,4},{24,8},{28,12},{1,17},{... | collective-permute-start | bytes 172040 | tf_op jit(solution)/shard_map/ppermute | solution.py:665
  441.0 2.1 copy-start.20
  441.0 3.3 copy-start.10
  444.3 2.5 copy-start.9
  (2 other events, 1.4 us)
Sparse Core Ops, SparseCore 0:
  135.7 170.4 all-reduce.12
  311.0 125.2 all-reduce.10
